TPU v7x, 32 devices: a whole 2x2x4 slice. The times are simulated.
32 devices in a mesh: batch: 16 (over z, y, x), heads: 2 (over core).
Axes of the slice: x: 2, y: 2, z: 4, core: 2. Of those that a mesh axis runs over, the one named last changes fastest.
Arguments:
- text_states: bfloat16 [64, 128, 768], P(('batch', 'heads')), may hold values from -6 to 6
- image_states: bfloat16 [64, 104, 1024], P(('batch', 'heads')), may hold values from -6 to 6
- caption_lengths: int32 [64], P('batch'), may hold values from 16 to 128, as said below
- region_counts: int32 [64], P('batch'), may hold values from 20 to 101, as said below
- text_query: bfloat16 [768, 1024], replicated, may hold values from -0.21875 to 0.21875
- text_key: bfloat16 [768, 1024], replicated, may hold values from -0.21875 to 0.21875
- text_value: bfloat16 [768, 1024], replicated, may hold values from -0.21875 to 0.21875
- text_output: bfloat16 [1024, 768], replicated, may hold values from -0.75 to 0.75
- text_up: bfloat16 [768, 3072], replicated, may hold values from -0.21875 to 0.21875
- text_down: bfloat16 [3072, 768], replicated, may hold values from -0.109375 to 0.109375
- text_gains: float32 [2, 768], replicated, may hold values from 0.25 to 1.75
- text_shifts: float32 [2, 768], replicated, may hold values from -1 to 1
- image_query: bfloat16 [1024, 1024], replicated, may hold values from -0.1875 to 0.1875
- image_key: bfloat16 [1024, 1024], replicated, may hold values from -0.1875 to 0.1875
- image_value: bfloat16 [1024, 1024], replicated, may hold values from -0.1875 to 0.1875
- image_output: bfloat16 [1024, 1024], replicated, may hold values from -0.75 to 0.75
- image_up: bfloat16 [1024, 1024], replicated, may hold values from -0.1875 to 0.1875
- image_down: bfloat16 [1024, 1024], replicated, may hold values from -0.1875 to 0.1875
- image_gains: float32 [2, 1024], replicated, may hold values from 0.25 to 1.75
- image_shifts: float32 [2, 1024], replicated, may hold values from -1 to 1
- text_upstream: bfloat16 [64, 128, 768], P(('batch', 'heads')), may hold values from -6 to 6
- image_upstream: bfloat16 [64, 104, 1024], P(('batch', 'heads')), may hold values from -6 to 6
Outputs:
- text_result: bfloat16 [64, 128, 768], P(('batch', 'heads'))
- image_result: bfloat16 [64, 104, 1024], P(('batch', 'heads'))
- text_states_grad: bfloat16 [64, 128, 768], P(('batch', 'heads'))
- image_states_grad: bfloat16 [64, 104, 1024], P(('batch', 'heads'))
- text_query_grad: float32 [768, 1024], P(('batch', 'heads'))
- text_key_grad: float32 [768, 1024], P(('batch', 'heads'))
- text_value_grad: float32 [768, 1024], P(('batch', 'heads'))
- text_output_grad: float32 [1024, 768], P(None, ('batch', 'heads'))
- text_up_grad: float32 [768, 3072], P(('batch', 'heads'))
- text_down_grad: float32 [3072, 768], P(None, ('batch', 'heads'))
- text_gains_grad: float32 [2, 768], P(None, ('batch', 'heads'))
- text_shifts_grad: float32 [2, 768], P(None, ('batch', 'heads'))
- image_query_grad: float32 [1024, 1024], P(('batch', 'heads'))
- image_key_grad: float32 [1024, 1024], P(('batch', 'heads'))
- image_value_grad: float32 [1024, 1024], P(('batch', 'heads'))
- image_output_grad: float32 [1024, 1024], P(None, ('batch', 'heads'))
- image_up_grad: float32 [1024, 1024], P(('batch', 'heads'))
- image_down_grad: float32 [1024, 1024], P(None, ('batch', 'heads'))
- image_gains_grad: float32 [2, 1024], P(None, ('batch', 'heads'))
- image_shifts_grad: float32 [2, 1024], P(None, ('batch', 'heads'))
Inputs may be any that keep to these rules, and one draw needn't show every extreme that they name: `caption_lengths`: some pair has exactly 128 caption tokens. `region_counts`: some pair has exactly 101 regions; region slots from a pair's count up to 104 are padding.
All inputs are finite; a program needn't handle non-finite values.
Results may differ from a plain program's by a relative error of at most 0.013.
Values may be sent and summed in bfloat16 or wider, within the bound.
A program may use at most 256 MiB of HBM per device.

v0:
```python
import functools
import math

import jax
import jax.numpy as jnp
from jax import lax
from jax.experimental import pallas as pl
from jax.experimental.pallas import tpu as pltpu
from jax.sharding import PartitionSpec as P

MESH_ID = pl.DeviceIdType.MESH
F32 = jnp.float32
BF16 = jnp.bfloat16
EPS = 1e-05
NEG = -1000000000.0
HEADS = 8
HEAD = 128
SCALE = 1.0 / math.sqrt(HEAD)
TILE = 256
CW = 256
LEFTS = (0, 1, 2, 3, 3, 3)
NT_DIMS = (((1,), (1,)), ((), ()))
TN_DIMS = (((0,), (0,)), ((), ()))
SLOTS = 6
G_RING, R_RING, Z_RING = 12, 12, 16
PRODUCED = ((1, 0), (1, 1), (1, 2), (0, 0), (0, 1), (0, 2), (1, 3), (0, 4), (0, 5), (0, 3), (1, 4), (1, 5))
SEQUENCE = (
    "i_qkv", "i_attend", "i_out", "i_ffn", "i_norm", "i_slope", "A0", "i_branch", "A1", "i_context", "t_q", "t_kv",
    "A2", "T0", "t_attend", "t_out", "T1", "t_ffn0", "t_ffn1", "t_ffn2", "T2", "t_norm", "A3", "t_slope0", "A4", "T3",
    "t_slope1", "A5", "T4", "t_slope2", "t_branch", "A6", "T5", "A7", "T6", "i_back", "A8", "T7", "t_context", "A9",
    "T8", "A10", "T9", "t_back", "A11", "T10", "A12", "T11", "A13", "T12", "i_final", "A14", "T13", "t_final", "A15",
    "T14", "T15", "T16", "T17", "T18", "T19",
)


def dot(a, b):
    return jnp.dot(a, b, preferred_element_type=F32)


def dot_nt(a, b):
    return lax.dot_general(a, b, NT_DIMS, preferred_element_type=F32)


def dot_tn(a, b):
    return lax.dot_general(a, b, TN_DIMS, preferred_element_type=F32)


def loop(n, body):
    def step(i, carry):
        body(i)
        return carry

    lax.fori_loop(0, n, step, 0)


def at(i, size):
    return pl.ds(pl.multiple_of(i * size, size), size)


def layer_kernel(dims, *refs):
    nz, ny, nx = dims
    refs = list(refs)

    def take(n):
        got = refs[:n]
        del refs[:n]
        return got

    cap_ref, reg_ref, xt_in, xi_in, ut_in, ui_in = take(6)
    w_in = [take(6), take(6)]
    gain_ref, shift_ref = take(2), take(2)
    res_t, res_i, sg_t, sg_i = take(4)
    w_out = [take(6), take(6)]
    norm_out = take(4)
    wbuf, x_t, x_i, raw_i, u_t, u_i = take(6)
    q_b, k_b, v_b = take(2), take(2), take(2)
    n1, inv, low, slope, acc, dctx, sums = take(2), take(2), take(2), take(2), take(2), take(2), take(2)
    lt = take(2)
    r_own, r_far = [take(6), take(6)], [take(6), take(6)]
    g_b, r1_b, r2_b, ru_b, rd_b = take(5)
    f_b = take(2)
    small, sv, sr = take(3)
    in_sem, w_sem, ex_s, ex_r, st_s, st_r, sm_s, sm_r = take(8)
    assert not refs

    b, h = lax.axis_index("batch"), lax.axis_index("heads")
    x, y, z = lax.rem(b, nx), lax.rem(lax.div(b, nx), ny), lax.div(b, nx * ny)

    def dev(zz, yy, xx):
        return ((zz * ny + yy) * nx + xx, h)

    partner, nbr_x, nbr_y = (b, 1 - h), dev(z, y, 1 - x), dev(z, 1 - y, x)
    barrier = pltpu.get_barrier_semaphore()
    for who in (partner, nbr_x, nbr_y):
        pl.semaphore_signal(barrier, inc=1, device_id=who, device_id_type=MESH_ID)
    for off in range(1, nz):
        pl.semaphore_signal(barrier, inc=1, device_id=dev(lax.rem(z + off, nz), y, x), device_id_type=MESH_ID)

    def remote(src, dst, ssem, rsem, who):
        return pltpu.make_async_remote_copy(
            src_ref=src, dst_ref=dst, send_sem=ssem, recv_sem=rsem, device_id=who, device_id_type=MESH_ID
        )

    T, I = 0, 1
    pieces = []

    def piece(name, ref, rows, cols):
        pieces.append((name, ref, rows, cols))

    td, ti = x_t.shape[1], x_i.shape[1]
    inner = q_b[0].shape[1]
    parts = w_in[T][1].shape[1] // 1024
    whole = lambda s, w: w_in[s][w]
    tu = lambda j: w_in[T][1].at[:, pl.ds(j * 1024, 1024)]
    tw = lambda j: w_in[T][0].at[pl.ds(j * 1024, 1024), :]
    piece("tk", whole(T, 4), td, inner)
    piece("tv", whole(T, 5), td, inner)
    piece("iq", whole(I, 3), ti, inner)
    piece("io", whole(I, 2), inner, ti)
    piece("iu", whole(I, 1), ti, ti)
    piece("id", whole(I, 0), ti, ti)
    piece("tq", whole(T, 3), td, inner)
    piece("ik", whole(I, 4), ti, inner)
    piece("iv", whole(I, 5), ti, inner)
    piece("to", whole(T, 2), inner, td)
    for j in range(parts):
        piece("tu%d" % j, tu(j), td, 1024)
        piece("td%d" % j, tw(j), 1024, td)
    piece("to", whole(T, 2), inner, td)
    for name, s, w in (("iq", I, 3), ("tk", T, 4), ("tv", T, 5), ("tq", T, 3), ("ik", I, 4), ("iv", I, 5)):
        rows = td if s == T else ti
        piece(name, whole(s, w), rows, inner)
    issued = [0]
    held = {}

    def weight_copy(k, slot):
        name, ref, rows, cols = pieces[k]
        return pltpu.make_async_copy(ref, wbuf.at[slot, pl.ds(0, rows), pl.ds(0, cols)], w_sem.at[slot])

    def issue(slot):
        if issued[0] < len(pieces):
            k = issued[0]
            issued[0] += 1
            weight_copy(k, slot).start()
            assert pieces[k][0] not in held
            held[pieces[k][0]] = [k, slot, False]

    def weight(name):
        k, slot, ready = held[name]
        if not ready:
            weight_copy(k, slot).wait()
            held[name][2] = True
        _, _, rows, cols = pieces[k]
        return wbuf.at[slot, pl.ds(0, rows), pl.ds(0, cols)]

    def release(name):
        k, slot, ready = held.pop(name)
        issue(slot)

    in_copies = [
        pltpu.make_async_copy(s, d, in_sem.at[i])
        for i, (s, d) in enumerate(((xt_in, x_t), (xi_in, raw_i.at[0]), (ut_in, u_t), (ui_in, raw_i.at[1])))
    ]
    in_copies[0].start()
    issue(0)
    in_copies[1].start()
    issue(1)
    issue(2)
    in_copies[3].start()
    in_copies[2].start()
    for slot in range(3, SLOTS):
        issue(slot)

    pairs_n, regions = raw_i.shape[1], raw_i.shape[2]
    cap = x_t.shape[0] // pairs_n
    pad = 112
    m_i, m_t = pairs_n * pad, x_t.shape[0]
    m_of, d_of = (m_t, m_i), (td, ti)
    x_of = (x_t, x_i)

    tail = pl.ds(m_i, x_i.shape[0] - m_i)
    for ref in (x_i, low[I], *r_own[I]):
        ref[tail, :] = jnp.zeros((x_i.shape[0] - m_i, ref.shape[1]), BF16)
    for ref in (*sums,):
        ref[...] = jnp.zeros(ref.shape, F32)

    def spread(src, dst):
        for p in range(pairs_n):
            dst[pl.ds(p * pad, regions), :] = src[p]
            dst[pl.ds(p * pad + regions, pad - regions), :] = jnp.zeros((pad - regions, dst.shape[1]), BF16)

    lengths = {
        T: [reg_ref[h * pairs_n + p] for p in range(pairs_n)],
        I: [cap_ref[h * pairs_n + p] for p in range(pairs_n)],
    }

    ex_left, ex_right = {}, {}
    n_left = max(LEFTS) + 1
    for s in (T, I):
        for l in range(n_left):
            k = s * n_left + l
            ex_left[s, l] = remote(
                lt[s].at[l, :, pl.ds(0, 256)], lt[s].at[l, :, pl.ds(256, 256)], ex_s.at[k], ex_r.at[k], partner
            )
        for w in range(6):
            k = 2 * n_left + s * 6 + w
            half = r_far[s][w].shape[1]
            ex_right[s, w] = remote(
                r_own[s][w].at[:, pl.ds(pl.multiple_of((1 - h) * half, 128), half)], r_far[s][w],
                ex_s.at[k], ex_r.at[k], partner,
            )
    arrived = set()
    entered = []

    def enter():
        if not entered:
            entered.append(1)
            pl.semaphore_wait(barrier, 3 + nz - 1)

    def send_left(s, l, src):
        def body(j):
            lt[s][l, at(j, TILE), pl.ds(0, 256)] = src[:, at(j, TILE)].T

        loop(d_of[s] // TILE, body)
        enter()
        ex_left[s, l].start()

    def send_right(s, w):
        enter()
        ex_right[s, w].start()

    def project(src, rows, w, dst):
        def body(j):
            dst[pl.ds(0, rows), at(j, TILE)] = dot(src[pl.ds(0, rows), :], w[:, at(j, TILE)]).astype(BF16)

        loop(w.shape[1] // TILE, body)

    def softmax(q, k, live):
        s = dot_nt(q, k) * SCALE
        mask = lax.broadcasted_iota(jnp.int32, s.shape, 1) < live
        s = jnp.where(mask, s, NEG)
        e = jnp.exp(s - jnp.max(s, axis=-1, keepdims=True))
        return e / jnp.sum(e, axis=-1, keepdims=True)

    span = (cap, pad)

    def rows_of(s, p):
        return pl.ds(p * span[s], span[s])

    def attend(s):
        o = 1 - s

        def body(i):
            cols = at(i, HEAD)
            for p in range(pairs_n):
                q, k = q_b[s][rows_of(s, p), cols], k_b[o][rows_of(o, p), cols]
                prob = softmax(q, k, lengths[s][p]).astype(BF16)
                r_own[s][2][rows_of(s, p), cols] = dot(prob, v_b[o][rows_of(o, p), cols]).astype(BF16)

        loop(HEADS, body)
        send_right(s, 2)

    def attend_back(s):
        o = 1 - s

        def body(i):
            cols = at(i, HEAD)
            for p in range(pairs_n):
                rq, rk = rows_of(s, p), rows_of(o, p)
                q, k, v, dc = q_b[s][rq, cols], k_b[o][rk, cols], v_b[o][rk, cols], dctx[s][rq, cols]
                prob = softmax(q, k, lengths[s][p])
                dp = dot_nt(dc, v)
                ds = (prob * (dp - jnp.sum(prob * dp, axis=-1, keepdims=True))).astype(BF16)
                r_own[s][3][rq, cols] = (dot(ds, k) * SCALE).astype(BF16)
                r_own[o][4][rk, cols] = (dot_tn(ds, q) * SCALE).astype(BF16)
                r_own[o][5][rk, cols] = dot_tn(prob.astype(BF16), dc).astype(BF16)

        loop(HEADS, body)
        send_right(s, 3)
        send_right(o, 4)
        send_right(o, 5)

    RB = 32

    def mean(v):
        return jnp.mean(v, axis=-1, keepdims=True)

    def sum8(v):
        return jnp.sum(v.reshape(v.shape[0] // 8, 8, v.shape[1]), axis=0)

    def norm_one(s):
        gain, shift = gain_ref[s][0:1, :], shift_ref[s][0:1, :]

        def body(i):
            r = at(i, RB)
            v = x_of[s][r, :].astype(F32) + acc[s][r, :]
            c = v - mean(v)
            iv = lax.rsqrt(mean(c * c) + EPS)
            n = c * iv
            n1[s][r, :] = n
            inv[s][r, :] = jnp.broadcast_to(iv, (RB, 128))
            low[s][r, :] = (n * gain + shift).astype(BF16)

        loop(m_of[s] // RB, body)
        send_left(s, 1, low[s])

    def norm_two(s, up_ref, res_ref):
        gain0, shift0 = gain_ref[s][0:1, :], shift_ref[s][0:1, :]
        gain, shift = gain_ref[s][1:2, :], shift_ref[s][1:2, :]

        def body(i):
            r = at(i, RB)
            v = n1[s][r, :] * gain0 + shift0 + acc[s][r, :]
            c = v - mean(v)
            iv = lax.rsqrt(mean(c * c) + EPS)
            n = c * iv
            up = up_ref[r, :].astype(F32)
            res_ref[r, :] = (n * gain + shift).astype(BF16)
            un = up * n
            sums[s][1] = sums[s][1] + sum8(un)
            sums[s][3] = sums[s][3] + sum8(up)
            u = up * gain
            d = iv * (u - mean(u) - n * mean(un * gain))
            acc[s][r, :] = d
            low[s][r, :] = d.astype(BF16)

        loop(m_of[s] // RB, body)
        send_left(s, 0, low[s])

    def norm_one_back(s):
        gain = gain_ref[s][0:1, :]

        def body(i):
            r = at(i, RB)
            g, n = acc[s][r, :], n1[s][r, :]
            gn = g * n
            sums[s][0] = sums[s][0] + sum8(gn)
            sums[s][2] = sums[s][2] + sum8(g)
            u = g * gain
            d = inv[s][r, 0:1] * (u - mean(u) - n * mean(gn * gain))
            acc[s][r, :] = d
            low[s][r, :] = d.astype(BF16)

        loop(m_of[s] // RB, body)
        send_left(s, 2, low[s])

    def out_project(s, w):
        m = m_of[s]

        def body(j):
            acc[s][pl.ds(0, m), at(j, TILE)] = dot(r_own[s][2][pl.ds(0, m), :], w[:, at(j, TILE)])

        loop(d_of[s] // TILE, body)

    def ffn(s, j, up_w, down_w):
        m, base = m_of[s], j * 1024

        def hidden(i):
            c = pl.ds(pl.multiple_of(base + i * TILE, TILE), TILE)
            v = dot(low[s][pl.ds(0, m), :], up_w[:, at(i, TILE)])
            half = 0.5 * (1.0 + lax.erf(v * (1.0 / math.sqrt(2.0))))
            r_own[s][0][pl.ds(0, m), c] = (v * half).astype(BF16)
            slope[s][pl.ds(0, m), c] = (half + v * jnp.exp(-0.5 * v * v) * (1.0 / math.sqrt(2.0 * math.pi))).astype(BF16)

        loop(1024 // TILE, hidden)

        def second(i):
            part = dot(r_own[s][0][pl.ds(0, m), pl.ds(base, 1024)], down_w[:, at(i, TILE)])
            if j == 0:
                acc[s][pl.ds(0, m), at(i, TILE)] = part
            else:
                acc[s][pl.ds(0, m), at(i, TILE)] += part

        loop(d_of[s] // TILE, second)

    def slope_back(s, j, down_w):
        m, base = m_of[s], j * 1024

        def body(i):
            c = pl.ds(pl.multiple_of(base + i * TILE, TILE), TILE)
            g = dot_nt(low[s][pl.ds(0, m), :], down_w[at(i, TILE), :])
            r_own[s][1][pl.ds(0, m), c] = (g * slope[s][pl.ds(0, m), c].astype(F32)).astype(BF16)

        loop(1024 // TILE, body)

    def back_add(s, src, cols, w):
        m = m_of[s]

        def body(i):
            acc[s][pl.ds(0, m), at(i, TILE)] += dot_nt(src[pl.ds(0, m), cols], w[at(i, TILE), :])

        loop(d_of[s] // TILE, body)

    def context_back(s, w):
        m = m_of[s]

        def body(i):
            dctx[s][pl.ds(0, m), at(i, TILE)] = dot_nt(low[s][pl.ds(0, m), :], w[at(i, TILE), :]).astype(BF16)

        loop(inner // TILE, body)

    def final(s, dst):
        def body(i):
            dst[at(i, RB), :] = acc[s][at(i, RB), :].astype(BF16)

        loop(m_of[s] // RB, body)

    def gather_rows(src, dst):
        for p in range(pairs_n):
            dst[p] = src[pl.ds(p * pad, regions), :]

    all_cols = pl.ds(0, 1024)

    def step(name):
        if name == "i_qkv":
            in_copies[0].wait()
            project(x_t, m_t, weight("tk"), k_b[T])
            release("tk")
            project(x_t, m_t, weight("tv"), v_b[T])
            release("tv")
            in_copies[1].wait()
            spread(raw_i.at[0], x_i)
            project(x_i, m_i, weight("iq"), q_b[I])
            release("iq")
        elif name == "i_attend":
            attend(I)
        elif name == "i_out":
            out_project(I, weight("io"))
            norm_one(I)
        elif name == "i_ffn":
            ffn(I, 0, weight("iu"), weight("id"))
            send_right(I, 0)
        elif name == "i_norm":
            in_copies[3].wait()
            spread(raw_i.at[1], u_i)
            norm_two(I, u_i, u_i)
            gather_rows(u_i, res_i)
        elif name == "i_slope":
            slope_back(I, 0, weight("id"))
            send_right(I, 1)
            release("id")
        elif name == "i_branch":
            back_add(I, r_own[I][1], all_cols, weight("iu"))
            release("iu")
            norm_one_back(I)
        elif name == "i_context":
            context_back(I, weight("io"))
            release("io")
            send_left(I, 3, x_i)
        elif name == "t_q":
            project(x_t, m_t, weight("tq"), q_b[T])
            release("tq")
            send_left(T, 3, x_t)
        elif name == "t_kv":
            project(x_i, m_i, weight("ik"), k_b[I])
            release("ik")
            project(x_i, m_i, weight("iv"), v_b[I])
            release("iv")
        elif name == "t_attend":
            attend(T)
        elif name == "t_out":
            out_project(T, weight("to"))
            release("to")
            norm_one(T)
        elif name.startswith("t_ffn"):
            j = int(name[-1])
            ffn(T, j, weight("tu%d" % j), weight("td%d" % j))
            if j == parts - 1:
                send_right(T, 0)
        elif name == "t_norm":
            in_copies[2].wait()
            norm_two(T, u_t, res_t)
        elif name.startswith("t_slope"):
            j = int(name[-1])
            slope_back(T, j, weight("td%d" % j))
            release("td%d" % j)
            if j == parts - 1:
                send_right(T, 1)
        elif name == "t_branch":
            for j in range(parts):
                back_add(T, r_own[T][1], pl.ds(j * 1024, 1024), weight("tu%d" % j))
                release("tu%d" % j)
            norm_one_back(T)
            small_fill()
        elif name == "t_context":
            context_back(T, weight("to"))
            release("to")
        elif name == "i_back":
            attend_back(I)
            back_add(I, r_own[I][3], all_cols, weight("iq"))
            release("iq")
            back_add(T, r_own[T][4], all_cols, weight("tk"))
            release("tk")
            back_add(T, r_own[T][5], all_cols, weight("tv"))
            release("tv")
        elif name == "t_back":
            attend_back(T)
        elif name == "i_final":
            back_add(I, r_own[I][4], all_cols, weight("ik"))
            release("ik")
            back_add(I, r_own[I][5], all_cols, weight("iv"))
            release("iv")
            final(I, u_i)
            gather_rows(u_i, sg_i)
        elif name == "t_final":
            back_add(T, r_own[T][3], all_cols, weight("tq"))
            release("tq")
            final(T, sg_t)
        elif name[0] == "A":
            for c in (2 * int(name[1:]), 2 * int(name[1:]) + 1):
                compute(c)
                s1(c).start()
        else:
            tick(int(name[1:]))

    small_copies = []

    def small_start(src, dst, i, who):
        c = remote(src, dst, sm_s.at[i], sm_r.at[i], who)
        c.start()
        small_copies.append(c)

    def small_fill():
        small[...] = jnp.zeros(small.shape, F32)
        for s in (T, I):
            for k in range(4):
                small[pl.ds(4 * s + k, 1), pl.ds(0, d_of[s])] = jnp.sum(sums[s][k], axis=0, keepdims=True)

    def small_step(i):
        if i == 0:
            small_start(small, sr.at[0], 0, partner)
        elif i == 1:
            small_copies[0].wait_recv()
            sv[0] = small[...] + sr[0]
            small_start(sv.at[0], sr.at[1], 1, nbr_x)
        elif i == 2:
            small_copies[1].wait_recv()
            sv[1] = sv[0] + sr[1]
            small_start(sv.at[1], sr.at[2], 2, nbr_y)
        elif i == 3:
            small_copies[2].wait_recv()
            sv[2] = sv[1] + sr[2]
            for off in range(1, nz):
                small_start(sv.at[2], sr.at[2 + off], 2 + off, dev(lax.rem(z + off, nz), y, x))
        elif i == 4:
            total = sv[2]
            for off in range(1, nz):
                small_copies[2 + off].wait_recv()
                total = total + sr[2 + off]
            wide = total.shape[1]
            me = b * 2 + h
            for s in (T, I):
                own = norm_out[2 * s].shape[1]
                mine = pltpu.roll(total, lax.rem(wide - me * own, wide), 1)
                norm_out[2 * s][...] = mine[4 * s : 4 * s + 2, :own]
                norm_out[2 * s + 1][...] = mine[4 * s + 2 : 4 * s + 4, :own]

    chunks = []
    for s, w in PRODUCED:
        for o in range(0, r_far[s][w].shape[1], CW):
            chunks.append((s, w, o, "xy"[len(chunks) % 2], len([1 for c in chunks if c[0] == s])))
    n = len(chunks)

    def bufs(c):
        rows = pl.ds(0, d_of[chunks[c][0]] // (nz * ny * nx))
        return (
            g_b.at[c % G_RING, :, :, :, rows], r1_b.at[c % R_RING, :, :, rows], r2_b.at[c % R_RING, :, rows],
            ru_b.at[c % Z_RING, :, rows], rd_b.at[c % Z_RING, :, rows],
        )

    def compute(c):
        s, w, o, way, _ = chunks[c]
        for copy, key in ((ex_left[s, LEFTS[w]], (0, s, LEFTS[w])), (ex_right[s, w], (1, s, w))):
            if key not in arrived:
                arrived.add(key)
                copy.wait_recv()
        blk = d_of[s] // (nz * ny * nx)
        size = ny * nx * blk
        half = r_far[s][w].shape[1]
        mine = pl.ds(pl.multiple_of(h * half + o, 128), CW)
        g = g_b.at[c % G_RING]

        def body(i):
            r = pl.ds(pl.multiple_of(i * size, 64), size)
            l = LEFTS[w]
            res = dot(lt[s][l, r, pl.ds(0, 256)], r_own[s][w][:, mine]) + dot(
                lt[s][l, r, pl.ds(256, 256)], r_far[s][w][:, pl.ds(o, CW)]
            )
            g[i, :, :, pl.ds(0, blk)] = res.astype(BF16).reshape(ny, nx, blk, CW)

        loop(nz, body)

    def add(dst, src):
        dst[...] = (dst[...].astype(F32) + src[...].astype(F32)).astype(BF16)

    def s1(c):
        g, r1 = bufs(c)[:2]
        if chunks[c][3] == "x":
            return remote(g.at[:, :, 1 - x], r1, st_s.at[0, c], st_r.at[0, c], nbr_x)
        return remote(g.at[:, 1 - y], r1, st_s.at[0, c], st_r.at[0, c], nbr_y)

    def s2(c):
        g, _, r2 = bufs(c)[:3]
        if chunks[c][3] == "x":
            return remote(g.at[:, 1 - y, x], r2, st_s.at[1, c], st_r.at[1, c], nbr_y)
        return remote(g.at[:, y, 1 - x], r2, st_s.at[1, c], st_r.at[1, c], nbr_x)

    def up(c, k):
        g, ru = bufs(c)[0], bufs(c)[3]
        rest = pl.ds(k + 1, nz - 1 - k)
        return remote(g.at[rest, y, x], ru.at[rest], st_s.at[2, c], st_r.at[2, c], dev(k + 1, y, x))

    def down(c, k):
        g, rd = bufs(c)[0], bufs(c)[4]
        rest = pl.ds(0, k)
        return remote(g.at[rest, y, x], rd.at[rest], st_s.at[3, c], st_r.at[3, c], dev(k - 1, y, x))

    def swap(c):
        s, w, o, _, k = chunks[c]
        out = w_out[s][w]
        half = out.shape[1] // 2
        return remote(
            f_b[s].at[k], out.at[:, pl.ds(pl.multiple_of(h * half + o, 128), CW)],
            st_s.at[4, c], st_r.at[4, c], partner,
        )

    def stage2(c):
        s1(c).wait_recv()
        g, r1 = bufs(c)[:2]

        def body(i):
            for j in range(2):
                add(g.at[i, j, x] if chunks[c][3] == "x" else g.at[i, y, j], r1.at[i, j])

        loop(nz, body)
        s2(c).start()

    def stage3(c):
        s2(c).wait_recv()
        g, _, r2 = bufs(c)[:3]
        loop(nz, lambda i: add(g.at[i, y, x], r2.at[i]))

        @pl.when(z == 0)
        def _():
            up(c, 0).start()

        @pl.when(z == nz - 1)
        def _():
            down(c, nz - 1).start()

    def hop(c, d):
        g, _, _, ru, rd = bufs(c)

        @pl.when(z == d)
        def _():
            up(c, d - 1).wait_recv()
            for t in range(d + 1, nz):
                add(g.at[t, y, x], ru.at[t])
            up(c, d).start()

        @pl.when(z == nz - 1 - d)
        def _():
            down(c, nz - d).wait_recv()
            for t in range(0, nz - 1 - d):
                add(g.at[t, y, x], rd.at[t])
            down(c, nz - 1 - d).start()

    def finish(c):
        g, _, _, ru, rd = bufs(c)
        s, w, o, _, idx = chunks[c]
        out = w_out[s][w]
        r, half = out.shape[0], out.shape[1] // 2
        cols = pl.ds(pl.multiple_of(h * half + o, 128), CW)
        for k in range(nz):

            @pl.when(z == k)
            def _(k=k):
                if k == nz - 1:
                    up(c, k - 1).wait_recv()
                if k == 0:
                    down(c, 1).wait_recv()
                total = g[k, y, x].astype(F32)
                if k > 0:
                    total = total + ru[k].astype(F32)
                if k < nz - 1:
                    total = total + rd[k].astype(F32)
                first, second = total[:r], total[r:]
                out[:, cols] = jnp.where(h == 0, first, second)
                f_b[s][idx] = jnp.where(h == 0, second, first)

        swap(c).start()
        s1(c).wait_send()
        s2(c).wait_send()
        for k in range(nz):

            @pl.when(z == k)
            def _(k=k):
                if k < nz - 1:
                    up(c, k).wait_send()
                if k > 0:
                    down(c, k).wait_send()

    pairs = n // 2
    small_from = 6

    def tick(t):
        for lag, stage in (
            (0, stage2), (1, stage3), *[(1 + d, functools.partial(hop, d=d)) for d in range(1, nz - 1)], (nz, finish)
        ):
            p = t - lag
            if 0 <= p < pairs:
                stage(2 * p)
                stage(2 * p + 1)
        if small_from <= t < small_from + 5:
            small_step(t - small_from)

    for name in SEQUENCE:
        step(name)

    for c in range(n):
        swap(c).wait_recv()
        swap(c).wait_send()
    for copy in (*ex_left.values(), *ex_right.values()):
        copy.wait_send()
    for copy in small_copies:
        copy.wait_send()


def layer(dims, lengths, states, upstream, weights, gains, shifts):
    nz, ny, nx = dims
    chips = nz * ny * nx
    xt, xi = states
    pairs, cap, td = xt.shape
    regions, ti = xi.shape[1:]
    xt, ut = xt.reshape(pairs * cap, td), upstream[0].reshape(pairs * cap, td)
    mt = pairs * cap
    fixed = 256
    inner = weights[0][3].shape[1]
    d_of = (td, ti)
    cols = [[w.shape[0], weights[s][1].shape[1], inner, inner, inner, inner] for s, w in ((0, weights[0][0]), (1, weights[1][0]))]
    V, DMA = pltpu.VMEM, pltpu.SemaphoreType.DMA
    rows_of = (mt, fixed)
    ti_blk = ti // chips
    counts = [sum(c // 2 // CW for c in cols[s]) for s in range(2)]
    n = sum(counts)
    act = lambda dt, width: [V((rows_of[s], width[s]), dt) for s in range(2)]
    scratch = [
        V((SLOTS, 1024, 1024), BF16),
        V((mt, td), BF16), V((fixed, ti), BF16), V((2, pairs, regions, ti), BF16), V((mt, td), BF16), V((fixed, ti), BF16),
        *act(BF16, (inner, inner)), *act(BF16, (inner, inner)), *act(BF16, (inner, inner)),
        *act(F32, d_of), *act(F32, (128, 128)), *act(BF16, d_of), *act(BF16, (cols[0][1], cols[1][1])),
        *act(F32, d_of), *act(BF16, (inner, inner)),
        *[V((4, 8, d), F32) for d in d_of],
        *[V((4, d, 512), BF16) for d in d_of],
        *[V((rows_of[s], c), BF16) for s in range(2) for c in cols[s]],
        *[V((rows_of[s], c // 2), BF16) for s in range(2) for c in cols[s]],
        V((G_RING, nz, ny, nx, ti_blk, CW), BF16),
        V((R_RING, nz, 2, ti_blk, CW), BF16),
        V((R_RING, nz, ti_blk, CW), BF16),
        V((Z_RING, nz, ti_blk, CW), BF16),
        V((Z_RING, nz, ti_blk, CW), BF16),
        *[V((counts[s], d_of[s] // chips // 2, CW), F32) for s in range(2)],
        V((8, max(d_of)), F32), V((3, 8, max(d_of)), F32), V((2 + nz, 8, max(d_of)), F32),
        DMA((4,)), DMA((SLOTS,)), DMA((20,)), DMA((20,)), DMA((5, n)), DMA((5, n)), DMA((2 + nz,)), DMA((2 + nz,)),
    ]
    hbm = pl.BlockSpec(memory_space=pl.ANY)
    vm = pl.BlockSpec(memory_space=pltpu.VMEM)
    smem = pl.BlockSpec(memory_space=pltpu.SMEM)
    sds = jax.ShapeDtypeStruct
    outs = [
        sds((mt, td), BF16), sds((pairs, regions, ti), BF16), sds((mt, td), BF16), sds((pairs, regions, ti), BF16),
        *[sds((d_of[s] // chips // 2, c), F32) for s in range(2) for c in cols[s]],
        *[sds((2, d_of[s] // chips // 2), F32) for s in range(2) for _ in range(2)],
    ]
    got = pl.pallas_call(
        functools.partial(layer_kernel, dims),
        out_shape=outs,
        in_specs=[smem, smem, *[hbm] * 4, *[hbm] * 12, *[vm] * 4],
        out_specs=[vm] * len(outs),
        scratch_shapes=scratch,
        compiler_params=pltpu.CompilerParams(
            collective_id=0, has_side_effects=True, vmem_limit_bytes=67043328
        ),
        name="co_layer",
    )(*lengths, xt, xi, ut, upstream[1], *weights[0], *weights[1], *gains, *shifts)
    return got


def matmul(row_values, weight):
    return jnp.dot(row_values, weight, preferred_element_type=F32)


def project_back(gradient, weight):
    return lax.dot_general(gradient, weight, (((1,), (1,)), ((), ())), preferred_element_type=F32)


def outer_sum(row_values, gradient):
    return lax.dot_general(row_values, gradient, (((0,), (0,)), ((), ())), preferred_element_type=F32)


def layer_norm(values, gain, shift):
    row_mean = jnp.mean(values, axis=-1, keepdims=True)
    centred = values - row_mean
    spread = jnp.mean(centred * centred, axis=-1, keepdims=True)
    inverse = lax.rsqrt(spread + EPS)
    normed = centred * inverse
    return (normed * gain + shift, normed, inverse)


def norm_back(gradient, normed, inverse, gain):
    scaled = gradient * gain
    first_mean = jnp.mean(scaled, axis=-1, keepdims=True)
    second_mean = jnp.mean(scaled * normed, axis=-1, keepdims=True)
    into = inverse * (scaled - first_mean - normed * second_mean)
    return (into, jnp.sum(gradient * normed, axis=0), jnp.sum(gradient, axis=0))


def gelu_value(values):
    return 0.5 * values * (1.0 + jax.scipy.special.erf(values / math.sqrt(2.0)))


def gelu_slope(values):
    return 0.5 * (1.0 + jax.scipy.special.erf(values / math.sqrt(2.0))) + values * jnp.exp(
        -0.5 * values * values
    ) / math.sqrt(2.0 * math.pi)


def attend(queries, key_rows, value_rows, lengths):
    score_scale = 1.0 / math.sqrt(queries.shape[-1])
    scores = jnp.einsum("bqhd,bkhd->bhqk", queries, key_rows, preferred_element_type=F32) * score_scale
    live_mask = lax.broadcasted_iota(jnp.int32, scores.shape, 3) < lengths[:, None, None, None]
    scores = jnp.where(live_mask, scores, NEG)
    weights = jnp.exp(scores - jnp.max(scores, axis=-1, keepdims=True))
    probability = weights / jnp.sum(weights, axis=-1, keepdims=True)
    context = jnp.einsum("bhqk,bkhd->bqhd", probability.astype(BF16), value_rows, preferred_element_type=F32)
    return context.astype(BF16), probability


def attend_back(queries, key_rows, value_rows, probability, context_grad):
    score_scale = 1.0 / math.sqrt(queries.shape[-1])
    value_grad = jnp.einsum(
        "bhqk,bqhd->bkhd", probability.astype(BF16), context_grad, preferred_element_type=F32
    )
    prob_grad = jnp.einsum("bqhd,bkhd->bhqk", context_grad, value_rows, preferred_element_type=F32)
    row_inner = jnp.sum(probability * prob_grad, axis=-1, keepdims=True)
    score_grad = (probability * (prob_grad - row_inner)).astype(BF16)
    query_grad = jnp.einsum("bhqk,bkhd->bqhd", score_grad, key_rows, preferred_element_type=F32) * score_scale
    key_grad = jnp.einsum("bhqk,bqhd->bkhd", score_grad, queries, preferred_element_type=F32) * score_scale
    return (query_grad.astype(BF16), key_grad.astype(BF16), value_grad.astype(BF16))


def stream_forward(row_values, context, out_weight, up_weight, down_weight, gains, shifts):
    attended = matmul(context, out_weight)
    first_out, normed_one, inverse_one = layer_norm(row_values.astype(F32) + attended, gains[0], shifts[0])
    first_low = first_out.astype(BF16)
    before = matmul(first_low, up_weight)
    active = gelu_value(before).astype(BF16)
    second_out, normed_two, inverse_two = layer_norm(
        first_out + matmul(active, down_weight), gains[1], shifts[1]
    )
    kept_state = (normed_one, inverse_one, first_low, before, active, normed_two, inverse_two)
    return (second_out.astype(BF16), kept_state)


def stream_back(upstream, kept_state, out_weight, up_weight, down_weight, gains):
    normed_one, inverse_one, first_low, before, active, normed_two, inverse_two = kept_state
    branch_grad, gain_two, shift_two = norm_back(upstream.astype(F32), normed_two, inverse_two, gains[1])
    branch_low = branch_grad.astype(BF16)
    active_grad = project_back(branch_low, down_weight)
    before_grad = (active_grad * gelu_slope(before)).astype(BF16)
    first_grad = project_back(before_grad, up_weight) + branch_grad
    sum_grad, gain_one, shift_one = norm_back(first_grad, normed_one, inverse_one, gains[0])
    sum_low = sum_grad.astype(BF16)
    context_grad = project_back(sum_low, out_weight).astype(BF16)
    return sum_grad, context_grad, branch_low, before_grad, sum_low, (gain_one, gain_two, shift_one, shift_two)


def make_local(mesh):
    devices = mesh.shape["batch"] * mesh.shape["heads"]

    def local(
        text_states, image_states, caption_lengths, region_counts,
        text_query, text_key, text_value, text_output, text_up, text_down, text_gains, text_shifts,
        image_query, image_key, image_value, image_output, image_up, image_down, image_gains, image_shifts,
        text_upstream, image_upstream,
    ):
        def parts(grads):
            down, up, out, query, key, value = grads
            return query, key, value, out.T, up, down.T

        if mesh.shape["batch"] == 16 and mesh.shape["heads"] == 2:
            text_weights = (text_down, text_up, text_output, text_query, text_key, text_value)
            image_weights = (image_down, image_up, image_output, image_query, image_key, image_value)
            got = layer(
                (4, 2, 2), (caption_lengths, region_counts), (text_states, image_states), (text_upstream, image_upstream),
                (text_weights, image_weights), (text_gains, image_gains), (text_shifts, image_shifts),
            )
            return (
                got[0].reshape(text_states.shape), got[1], got[2].reshape(text_states.shape), got[3],
                *parts(got[4:10]), got[16], got[17], *parts(got[10:16]), got[18], got[19],
            )
        pair_count, cap_len, text_width = text_states.shape
        region_len, image_width = image_states.shape[1:]
        text_rows = text_states.reshape(pair_count * cap_len, text_width)
        image_rows = image_states.reshape(pair_count * region_len, image_width)
        core = lax.axis_index("heads")
        captions = lax.dynamic_slice(caption_lengths, (core * pair_count,), (pair_count,))
        regions = lax.dynamic_slice(region_counts, (core * pair_count,), (pair_count,))

        def heads_of(row_values, weight, length):
            return matmul(row_values, weight).astype(BF16).reshape(pair_count, length, HEADS, HEAD)

        tq, tk, tv = (heads_of(text_rows, w, cap_len) for w in (text_query, text_key, text_value))
        iq, ik, iv = (heads_of(image_rows, w, region_len) for w in (image_query, image_key, image_value))
        text_context, text_prob = attend(tq, ik, iv, regions)
        image_context, image_prob = attend(iq, tk, tv, captions)
        flat = lambda v: v.reshape(v.shape[0] * v.shape[1], -1)
        text_result, text_kept = stream_forward(
            text_rows, flat(text_context), text_output, text_up, text_down, text_gains, text_shifts
        )
        image_result, image_kept = stream_forward(
            image_rows, flat(image_context), image_output, image_up, image_down, image_gains, image_shifts
        )
        t_sum, t_cgrad, t_branch, t_zgrad, t_slow, t_small = stream_back(
            text_upstream.reshape(text_rows.shape), text_kept, text_output, text_up, text_down, text_gains
        )
        i_sum, i_cgrad, i_branch, i_zgrad, i_slow, i_small = stream_back(
            image_upstream.reshape(image_rows.shape), image_kept, image_output, image_up, image_down, image_gains
        )
        g_tq, g_ik, g_iv = attend_back(tq, ik, iv, text_prob, t_cgrad.reshape(tq.shape))
        g_iq, g_tk, g_tv = attend_back(iq, tk, tv, image_prob, i_cgrad.reshape(iq.shape))
        g_tq, g_tk, g_tv, g_iq, g_ik, g_iv = (flat(v) for v in (g_tq, g_tk, g_tv, g_iq, g_ik, g_iv))
        text_in = t_sum + project_back(g_tq, text_query) + project_back(g_tk, text_key) + project_back(g_tv, text_value)
        image_in = (
            i_sum + project_back(g_iq, image_query) + project_back(g_ik, image_key) + project_back(g_iv, image_value)
        )
        tl = (t_branch, text_kept[2], t_slow, text_rows)
        tr = (text_kept[4], t_zgrad, flat(text_context), g_tq, g_tk, g_tv)
        il = (i_branch, image_kept[2], i_slow, image_rows)
        ir = (image_kept[4], i_zgrad, flat(image_context), g_iq, g_ik, g_iv)
        wide = max(text_width, image_width)
        small = jnp.stack([jnp.pad(v, (0, wide - v.shape[0])) for v in t_small + i_small])
        me = lax.axis_index("batch") * mesh.shape["heads"] + core

        scatter = lambda v: lax.psum_scatter(v, ("batch", "heads"), scatter_dimension=0, tiled=True)
        text_grads = [scatter(outer_sum(tl[l], r)) for l, r in zip(LEFTS, tr)]
        image_grads = [scatter(outer_sum(il[l], r)) for l, r in zip(LEFTS, ir)]
        total = lax.psum(small, ("batch", "heads"))
        t_own, i_own = text_width // devices, image_width // devices
        t_norm = lax.dynamic_slice(total, (0, me * t_own), (4, t_own))
        i_norm = lax.dynamic_slice(total, (4, me * i_own), (4, i_own))
        return (
            text_result.reshape(text_states.shape),
            image_result.reshape(image_states.shape),
            text_in.astype(BF16).reshape(text_states.shape),
            image_in.astype(BF16).reshape(image_states.shape),
            *parts(text_grads), t_norm[:2], t_norm[2:],
            *parts(image_grads), i_norm[:2], i_norm[2:],
        )

    return local


def solution(mesh):
    rows = P(("batch", "heads"), None, None)
    first, second = P(("batch", "heads"), None), P(None, ("batch", "heads"))
    grads = (first, first, first, second, first, second, second, second)
    return jax.shard_map(
        make_local(mesh),
        mesh=mesh,
        in_specs=(rows, rows, P("batch"), P("batch"), *[P()] * 16, rows, rows),
        out_specs=(rows, rows, rows, rows, *grads, *grads),
        check_vma=False,
    )
```

profile of v0, /device:TPU:0, one launch (start us, length us, event | category | flops | bytes accessed | tf_op | source)
XLA Modules:
  0.0 203.7 jit_solution(1224945164061275655)
XLA Ops:
  0.7 186.5 %co_layer.1 = (bf16[256,768]{1,0:T(8,128)(2,1)}, bf16[2,104,1024]{2,1,0:T(8,128)(2,1)}, bf16[256,768]{1,0:T(8,128)(2,1)}, bf16[2,104,1024]{2,1,0:T(8,128)(2,1)},...) custom-call(s32[4]{0:T(128)} %refs_0_.1, ...), custom_call_target="tpu_custom_call" | custom-call | tf_op jit(solution)/shard_map/co_layer/pallas_call | solution.py:775
  187.1 0.0 copy-start
  187.2 0.0 copy-start.12
  187.2 0.0 copy-start.11
  187.2 0.0 copy-start.10
  187.2 0.0 copy-start.9
  187.2 0.0 copy-start.2
  187.2 1.8 copy.62
  189.1 0.0 copy-start.1
  189.1 0.0 copy-start.15
  189.1 0.0 copy-start.8
  189.1 1.8 copy.63
  190.9 1.8 copy.64
  192.7 0.0 copy-done
  192.7 0.0 copy-start.13
  192.8 0.8 copy.65
  193.5 0.0 copy-done.12
  193.5 0.6 copy.66
  194.2 0.0 copy-done.11
  194.2 0.6 copy.67
  194.8 0.0 copy-done.10
  194.8 0.6 copy.68
  195.4 0.0 copy-done.9
  195.4 0.6 copy.69
  196.1 0.0 copy-done.2
  196.1 0.7 copy.70
  196.8 0.0 copy-done.1
  196.8 0.7 copy.71
  197.5 0.0 copy-done.16
  197.5 0.6 copy.72
  198.1 0.0 copy-done.15
  198.1 0.6 copy.73
  198.7 0.0 copy-done.8
  198.7 0.7 copy.74
  199.3 0.0 copy-done.7
  199.3 0.7 copy.75
  200.0 0.0 copy-done.6
  200.0 0.7 copy.76
  200.6 0.0 copy-done.5
  200.6 0.7 copy.77
  201.3 0.0 copy-done.4
  201.3 0.7 copy.78
  201.9 0.0 copy-done.3
  201.9 0.7 copy.79
  202.6 0.0 copy-done.14
  202.6 0.6 copy.80
  203.2 0.0 copy-done.13
  203.2 0.6 copy.81
  (7 shorter events, 0.0 us)
Async XLA Ops:
  187.1 5.6 %copy-start = (bf16[2,104,1024]{2,1,0:T(8,128)(2,1)S(1)}, bf16[2,104,1024]{2,1,0:T(8,128)(2,1)}, u32[]{:S(2)}) copy-start(bf16[2,104,1024]{2,1,0:T(8,128)(2,1)} %get-tuple-element.83) | copy-start | bytes 1277956
  187.2 6.4 %copy-start.12 = (f32[24,1024]{1,0:T(8,128)S(1)}, f32[24,1024]{1,0:T(8,128)}, u32[]{:S(2)}) copy-start(f32[24,1024]{1,0:T(8,128)} %get-tuple-element.84) | copy-start | bytes 294916
  187.2 7.0 %copy-start.11 = (f32[24,1024]{1,0:T(8,128)S(1)}, f32[24,1024]{1,0:T(8,128)}, u32[]{:S(2)}) copy-start(f32[24,1024]{1,0:T(8,128)} %get-tuple-element.85) | copy-start | bytes 294916
  187.2 7.6 %copy-start.10 = (f32[24,1024]{1,0:T(8,128)S(1)}, f32[24,1024]{1,0:T(8,128)}, u32[]{:S(2)}) copy-start(f32[24,1024]{1,0:T(8,128)} %get-tuple-element.86) | copy-start | bytes 294916
  187.2 8.3 %copy-start.9 = (f32[24,1024]{1,0:T(8,128)S(1)}, f32[24,1024]{1,0:T(8,128)}, u32[]{:S(2)}) copy-start(f32[24,1024]{1,0:T(8,128)} %get-tuple-element.47) | copy-start | bytes 294916
  187.2 8.9 %copy-start.2 = (f32[24,3072]{1,0:T(8,128)S(1)}, f32[24,3072]{1,0:T(8,128)}, u32[]{:S(2)}) copy-start(f32[24,3072]{1,0:T(8,128)} %get-tuple-element.88) | copy-start | bytes 884740
  189.1 7.8 %copy-start.1 = (f32[24,3072]{1,0:T(8,128)S(1)}, f32[24,3072]{1,0:T(8,128)}, u32[]{:S(2)}) copy-start(f32[24,3072]{1,0:T(8,128)} %get-tuple-element.49) | copy-start | bytes 884740
  189.1 8.5 %copy-start.16 = (f32[2,24]{1,0:T(2,128)S(1)}, f32[2,24]{1,0:T(2,128)}, u32[]{:S(2)}) copy-start(f32[2,24]{1,0:T(2,128)} %get-tuple-element.90) | copy-start | bytes 580
  189.1 9.0 %copy-start.15 = (f32[2,24]{1,0:T(2,128)S(1)}, f32[2,24]{1,0:T(2,128)}, u32[]{:S(2)}) copy-start(f32[2,24]{1,0:T(2,128)} %get-tuple-element.91) | copy-start | bytes 580
  189.1 9.6 %copy-start.8 = (f32[32,1024]{1,0:T(8,128)S(1)}, f32[32,1024]{1,0:T(8,128)}, u32[]{:S(2)}) copy-start(f32[32,1024]{1,0:T(8,128)} %get-tuple-element.92) | copy-start | bytes 393220
  190.9 8.4 %copy-start.7 = (f32[32,1024]{1,0:T(8,128)S(1)}, f32[32,1024]{1,0:T(8,128)}, u32[]{:S(2)}) copy-start(f32[32,1024]{1,0:T(8,128)} %get-tuple-element.93) | copy-start | bytes 393220
  190.9 9.1 %copy-start.6 = (f32[32,1024]{1,0:T(8,128)S(1)}, f32[32,1024]{1,0:T(8,128)}, u32[]{:S(2)}) copy-start(f32[32,1024]{1,0:T(8,128)} %get-tuple-element.94) | copy-start | bytes 393220
  190.9 9.7 %copy-start.5 = (f32[32,1024]{1,0:T(8,128)S(1)}, f32[32,1024]{1,0:T(8,128)}, u32[]{:S(2)}) copy-start(f32[32,1024]{1,0:T(8,128)} %get-tuple-element.55) | copy-start | bytes 393220
  192.7 8.6 %copy-start.4 = (f32[32,1024]{1,0:T(8,128)S(1)}, f32[32,1024]{1,0:T(8,128)}, u32[]{:S(2)}) copy-start(f32[32,1024]{1,0:T(8,128)} %get-tuple-element.96) | copy-start | bytes 393220
  192.7 9.2 %copy-start.3 = (f32[32,1024]{1,0:T(8,128)S(1)}, f32[32,1024]{1,0:T(8,128)}, u32[]{:S(2)}) copy-start(f32[32,1024]{1,0:T(8,128)} %get-tuple-element.57) | copy-start | bytes 393220
  192.7 9.9 %copy-start.14 = (f32[2,32]{1,0:T(2,128)S(1)}, f32[2,32]{1,0:T(2,128)}, u32[]{:S(2)}) copy-start(f32[2,32]{1,0:T(2,128)} %get-tuple-element.98) | copy-start | bytes 772
  192.7 10.4 %copy-start.13 = (f32[2,32]{1,0:T(2,128)S(1)}, f32[2,32]{1,0:T(2,128)}, u32[]{:S(2)}) copy-start(f32[2,32]{1,0:T(2,128)} %get-tuple-element.99) | copy-start | bytes 772
where the time goes:
time: 204 us
  Pallas kernels  186 us (91%)
  local copies, waits for them, and re-layouts  16.5 us (8%)
    pallas_call x1, Pallas kernels, layer(): pl.pallas_call(functools.partial(layer_kernel, dims), out_shape=outs, in_...  186 us
    unnamed x54, local copies, waits for them, and re-layouts  16.5 us

commit v1 on v0

--- a/solution.py
+++ b/solution.py
@@ -726,6 +726,25 @@
         copy.wait_send()
 
 
+def hand_over(turned, *refs):
+    n = (len(refs) - 1 - len(turned)) // 2
+    ins, outs, scratch, sem = refs[:n], refs[n : 2 * n], refs[2 * n : -1], refs[-1]
+    copies = []
+
+    def send(i, src):
+        copies.append(pltpu.make_async_copy(src, outs[i], sem.at[i]))
+        copies[-1].start()
+
+    for i in range(n):
+        if i not in turned:
+            send(i, ins[i])
+    for i, ref in zip(turned, scratch):
+        ref[...] = ins[i][...].T
+        send(i, ref)
+    for c in copies:
+        c.wait()
+
+
 def layer(dims, lengths, states, upstream, weights, gains, shifts):
     nz, ny, nx = dims
     chips = nz * ny * nx
@@ -772,6 +791,7 @@
         *[sds((d_of[s] // chips // 2, c), F32) for s in range(2) for c in cols[s]],
         *[sds((2, d_of[s] // chips // 2), F32) for s in range(2) for _ in range(2)],
     ]
+    turned = (4, 6, 10, 12)
     got = pl.pallas_call(
         functools.partial(layer_kernel, dims),
         out_shape=outs,
@@ -783,7 +803,15 @@
         ),
         name="co_layer",
     )(*lengths, xt, xi, ut, upstream[1], *weights[0], *weights[1], *gains, *shifts)
-    return got
+    n = len(got)
+    return pl.pallas_call(
+        functools.partial(hand_over, turned),
+        out_shape=[sds(v.shape[::-1] if i in turned else v.shape, v.dtype) for i, v in enumerate(outs)],
+        in_specs=[vm] * n,
+        out_specs=[hbm] * n,
+        scratch_shapes=[*[V(outs[i].shape[::-1], F32) for i in turned], DMA((n,))],
+        name="hand_over",
+    )(*got)
 
 
 def matmul(row_values, weight):
@@ -884,9 +912,13 @@
         image_query, image_key, image_value, image_output, image_up, image_down, image_gains, image_shifts,
         text_upstream, image_upstream,
     ):
+        def named(grads):
+            down, up, out, query, key, value = grads
+            return query, key, value, out, up, down
+
         def parts(grads):
             down, up, out, query, key, value = grads
-            return query, key, value, out.T, up, down.T
+            return named((down.T, up, out.T, query, key, value))
 
         if mesh.shape["batch"] == 16 and mesh.shape["heads"] == 2:
             text_weights = (text_down, text_up, text_output, text_query, text_key, text_value)
@@ -897,7 +929,7 @@
             )
             return (
                 got[0].reshape(text_states.shape), got[1], got[2].reshape(text_states.shape), got[3],
-                *parts(got[4:10]), got[16], got[17], *parts(got[10:16]), got[18], got[19],
+                *named(got[4:10]), got[16], got[17], *named(got[10:16]), got[18], got[19],
             )
         pair_count, cap_len, text_width = text_states.shape
         region_len, image_width = image_states.shape[1:]

time: 204 us -> 199 us (0.975)
  local copies, waits for them, and re-layouts: 16.5 us -> 6.88 us
  Pallas kernels: 186 us -> 191 us
    unnamed x54 -> x6, local copies, waits for them, and re-layouts: 16.5 us -> 6.88 us
    pallas_call x0 -> x1, Pallas kernels: none -> 4.7 us  [layer(): pl.pallas_call(functools.partial(hand_over, turned), out_shape=[sds(v.sha...]
where the time goes in v1:
time: 199 us
  Pallas kernels  191 us (96%)
  local copies, waits for them, and re-layouts  6.88 us (3%)
    pallas_call x1, Pallas kernels, layer(): pl.pallas_call(functools.partial(layer_kernel, dims), out_shape=outs, in_...  187 us
    unnamed x6, local copies, waits for them, and re-layouts  6.88 us
    pallas_call x1, Pallas kernels, layer(): pl.pallas_call(functools.partial(hand_over, turned), out_shape=[sds(v.sha...  4.7 us

profile of v1, /device:TPU:0, one launch (start us, length us, event | category | flops | bytes accessed | tf_op | source)
XLA Modules:
  0.0 198.8 jit_solution(6949794061676441067)
XLA Ops:
  0.7 186.5 %co_layer.1 = (bf16[256,768]{1,0:T(8,128)(2,1)}, bf16[2,104,1024]{2,1,0:T(8,128)(2,1)}, bf16[256,768]{1,0:T(8,128)(2,1)}, bf16[2,104,1024]{2,1,0:T(8,128)(2,1)},...) custom-call(s32[4]{0:T(128)} %refs_0_.1, ...), custom_call_target="tpu_custom_call" | custom-call | tf_op jit(solution)/shard_map/co_layer/pallas_call | solution.py:795
  187.2 4.7 %hand_over.1 = (bf16[256,768]{1,0:T(8,128)(2,1)}, bf16[2,104,1024]{2,1,0:T(8,128)(2,1)}, bf16[256,768]{1,0:T(8,128)(2,1)}, bf16[2,104,1024]{2,1,0:T(8,128)(2,1)}...) custom-call(bf16[256,768]{1,0:T(8,128)(2,1)} %get-tuple-element.60.r, ...), custom_call_target="tpu_custom_call" | custom-call | tf_op jit(solution)/shard_map/hand_over/pallas_call | solution.py:807
  191.9 0.0 copy-start
  191.9 2.0 copy.42
  193.9 1.9 copy.44
  195.7 1.9 copy.45
  197.6 0.0 copy-done
  197.6 1.2 copy.43
Async XLA Ops:
  191.9 5.7 %copy-start = (f32[3072,24]{1,0:T(8,128)S(1)}, f32[3072,24]{1,0:T(8,128)}, u32[]{:S(2)}) copy-start(f32[3072,24]{1,0:T(8,128)} %get-tuple-element.109) | copy-start | bytes 884740

commit v2 on v0

--- a/solution.py
+++ b/solution.py
@@ -22,14 +22,17 @@
 NT_DIMS = (((1,), (1,)), ((), ()))
 TN_DIMS = (((0,), (0,)), ((), ()))
 SLOTS = 6
-G_RING, R_RING, Z_RING = 12, 12, 16
+UNROLL = 2
+HEAD_GROUP = 2
+G_RING, R_RING, Z_RING = 12, 12, 12
+LATE = (1, 2, 5, 6, 8, 11, 13, 14, 16, 17, 19, 20, 23, 24, 25, 26, 28, 29)
 PRODUCED = ((1, 0), (1, 1), (1, 2), (0, 0), (0, 1), (0, 2), (1, 3), (0, 4), (0, 5), (0, 3), (1, 4), (1, 5))
 SEQUENCE = (
-    "i_qkv", "i_attend", "i_out", "i_ffn", "i_norm", "i_slope", "A0", "i_branch", "A1", "i_context", "t_q", "t_kv",
-    "A2", "T0", "t_attend", "t_out", "T1", "t_ffn0", "t_ffn1", "t_ffn2", "T2", "t_norm", "A3", "t_slope0", "A4", "T3",
-    "t_slope1", "A5", "T4", "t_slope2", "t_branch", "A6", "T5", "A7", "T6", "i_back", "A8", "T7", "t_context", "A9",
-    "T8", "A10", "T9", "t_back", "A11", "T10", "A12", "T11", "A13", "T12", "i_final", "A14", "T13", "t_final", "A15",
-    "T14", "T15", "T16", "T17", "T18", "T19",
+    "i_qkv", "i_attend", "i_out", "i_ffn", "i_norm", "A0", "i_slope", "i_branch", "i_context", "A1", "t_q", "t_kv",
+    "t_attend", "T0", "A2", "t_out", "t_ffn0", "t_ffn1", "T1", "t_ffn2", "t_norm", "A3", "T2", "t_slope0", "A4", "T3",
+    "A5", "t_slope1", "t_slope2", "T4", "A6", "t_branch", "T5", "A7", "T6", "A8", "i_back", "T7", "A9", "t_context",
+    "T8", "A10", "t_back", "T9", "i_final", "A11", "t_final", "T10", "A12", "T11", "A13", "T12", "A14", "T13", "T14",
+    "A15", "T15", "T16", "T17", "T18", "T19",
 )
 
 
@@ -45,16 +48,24 @@
     return lax.dot_general(a, b, TN_DIMS, preferred_element_type=F32)
 
 
-def loop(n, body):
+def loop(n, body, unroll=None):
+    u = min(n, unroll or UNROLL)
+
     def step(i, carry):
-        body(i)
+        for k in range(u):
+            body(i * u + k)
         return carry
 
-    lax.fori_loop(0, n, step, 0)
+    if n == u:
+        step(0, 0)
+    else:
+        lax.fori_loop(0, n // u, step, 0)
+        for k in range(n - n % u, n):
+            body(k)
 
 
 def at(i, size):
-    return pl.ds(pl.multiple_of(i * size, size), size)
+    return pl.ds(i * size if isinstance(i, int) else pl.multiple_of(i * size, size), size)
 
 
 def layer_kernel(dims, *refs):
@@ -72,9 +83,9 @@
     res_t, res_i, sg_t, sg_i = take(4)
     w_out = [take(6), take(6)]
     norm_out = take(4)
-    wbuf, x_t, x_i, raw_i, u_t, u_i = take(6)
+    wbuf, x_t, x_i = take(3)
     q_b, k_b, v_b = take(2), take(2), take(2)
-    n1, inv, low, slope, acc, dctx, sums = take(2), take(2), take(2), take(2), take(2), take(2), take(2)
+    n1, inv, low, acc, dctx, sums = take(2), take(2), take(2), take(2), take(2), take(2)
     lt = take(2)
     r_own, r_far = [take(6), take(6)], [take(6), take(6)]
     g_b, r1_b, r2_b, ru_b, rd_b = take(5)
@@ -82,6 +93,7 @@
     small, sv, sr = take(3)
     in_sem, w_sem, ex_s, ex_r, st_s, st_r, sm_s, sm_r = take(8)
     assert not refs
+    u_t, u_i = dctx[0].at[:, pl.ds(0, x_t.shape[1])], dctx[1]
 
     b, h = lax.axis_index("batch"), lax.axis_index("heads")
     x, y, z = lax.rem(b, nx), lax.rem(lax.div(b, nx), ny), lax.div(b, nx * ny)
@@ -157,23 +169,37 @@
         k, slot, ready = held.pop(name)
         issue(slot)
 
+    pairs_n, regions = xi_in.shape[:2]
+    pad = 112
+
+    def image_rows(src, dst, k):
+        return [
+            pltpu.make_async_copy(src.at[p], dst.at[pl.ds(p * pad, regions), :], in_sem.at[k + p]) for p in range(pairs_n)
+        ]
+
+    def start(copies):
+        for c in copies:
+            c.start()
+
+    def wait(copies):
+        for c in copies:
+            c.wait()
+
     in_copies = [
-        pltpu.make_async_copy(s, d, in_sem.at[i])
-        for i, (s, d) in enumerate(((xt_in, x_t), (xi_in, raw_i.at[0]), (ut_in, u_t), (ui_in, raw_i.at[1])))
+        [pltpu.make_async_copy(xt_in, x_t, in_sem.at[0])], image_rows(xi_in, x_i, 2),
+        [pltpu.make_async_copy(ut_in, u_t, in_sem.at[1])], image_rows(ui_in, u_i, 2 + pairs_n),
     ]
-    in_copies[0].start()
+    start(in_copies[0])
     issue(0)
-    in_copies[1].start()
+    start(in_copies[1])
     issue(1)
     issue(2)
-    in_copies[3].start()
-    in_copies[2].start()
+    start(in_copies[3])
+    start(in_copies[2])
     for slot in range(3, SLOTS):
         issue(slot)
 
-    pairs_n, regions = raw_i.shape[1], raw_i.shape[2]
     cap = x_t.shape[0] // pairs_n
-    pad = 112
     m_i, m_t = pairs_n * pad, x_t.shape[0]
     m_of, d_of = (m_t, m_i), (td, ti)
     x_of = (x_t, x_i)
@@ -184,10 +210,9 @@
     for ref in (*sums,):
         ref[...] = jnp.zeros(ref.shape, F32)
 
-    def spread(src, dst):
+    for ref in (x_i, u_i):
         for p in range(pairs_n):
-            dst[pl.ds(p * pad, regions), :] = src[p]
-            dst[pl.ds(p * pad + regions, pad - regions), :] = jnp.zeros((pad - regions, dst.shape[1]), BF16)
+            ref[pl.ds(p * pad + regions, pad - regions), :] = jnp.zeros((pad - regions, ref.shape[1]), BF16)
 
     lengths = {
         T: [reg_ref[h * pairs_n + p] for p in range(pairs_n)],
@@ -235,47 +260,62 @@
 
         loop(w.shape[1] // TILE, body)
 
-    def softmax(q, k, live):
-        s = dot_nt(q, k) * SCALE
-        mask = lax.broadcasted_iota(jnp.int32, s.shape, 1) < live
-        s = jnp.where(mask, s, NEG)
-        e = jnp.exp(s - jnp.max(s, axis=-1, keepdims=True))
-        return e / jnp.sum(e, axis=-1, keepdims=True)
+    def softmaxes(parts_of):
+        scores = [dot_nt(q, k) * SCALE for q, k, _ in parts_of]
+        scores = [
+            jnp.where(lax.broadcasted_iota(jnp.int32, v.shape, 1) < live, v, NEG)
+            for v, (_, _, live) in zip(scores, parts_of)
+        ]
+        tops = [jnp.max(v, axis=-1, keepdims=True) for v in scores]
+        exps = [jnp.exp(v - t) for v, t in zip(scores, tops)]
+        totals = [jnp.sum(e, axis=-1, keepdims=True) for e in exps]
+        return [e / t for e, t in zip(exps, totals)]
 
     span = (cap, pad)
 
     def rows_of(s, p):
         return pl.ds(p * span[s], span[s])
 
+    def units(i):
+        return [(at(i * HEAD_GROUP + k, HEAD), p) for k in range(HEAD_GROUP) for p in range(pairs_n)]
+
     def attend(s):
         o = 1 - s
 
         def body(i):
-            cols = at(i, HEAD)
-            for p in range(pairs_n):
-                q, k = q_b[s][rows_of(s, p), cols], k_b[o][rows_of(o, p), cols]
-                prob = softmax(q, k, lengths[s][p]).astype(BF16)
-                r_own[s][2][rows_of(s, p), cols] = dot(prob, v_b[o][rows_of(o, p), cols]).astype(BF16)
-
-        loop(HEADS, body)
+            group = units(i)
+            probs = softmaxes(
+                [(q_b[s][rows_of(s, p), c], k_b[o][rows_of(o, p), c], lengths[s][p]) for c, p in group]
+            )
+            got = [dot(prob.astype(BF16), v_b[o][rows_of(o, p), c]) for prob, (c, p) in zip(probs, group)]
+            for g, (c, p) in zip(got, group):
+                r_own[s][2][rows_of(s, p), c] = g.astype(BF16)
+
+        loop(HEADS // HEAD_GROUP, body, 1)
         send_right(s, 2)
 
     def attend_back(s):
         o = 1 - s
 
         def body(i):
-            cols = at(i, HEAD)
-            for p in range(pairs_n):
+            group = units(i)
+            qs = [q_b[s][rows_of(s, p), c] for c, p in group]
+            ks = [k_b[o][rows_of(o, p), c] for c, p in group]
+            dcs = [dctx[s][rows_of(s, p), c] for c, p in group]
+            dps = [dot_nt(dc, v_b[o][rows_of(o, p), c]) for dc, (c, p) in zip(dcs, group)]
+            probs = softmaxes([(q, k, lengths[s][p]) for q, k, (_, p) in zip(qs, ks, group)])
+            dvs = [dot_tn(prob.astype(BF16), dc) for prob, dc in zip(probs, dcs)]
+            inner_sums = [jnp.sum(prob * dp, axis=-1, keepdims=True) for prob, dp in zip(probs, dps)]
+            dss = [(prob * (dp - t)).astype(BF16) for prob, dp, t in zip(probs, dps, inner_sums)]
+            dqs = [dot(ds, k) * SCALE for ds, k in zip(dss, ks)]
+            dks = [dot_tn(ds, q) * SCALE for ds, q in zip(dss, qs)]
+            for (c, p), dq, dk, dv in zip(group, dqs, dks, dvs):
                 rq, rk = rows_of(s, p), rows_of(o, p)
-                q, k, v, dc = q_b[s][rq, cols], k_b[o][rk, cols], v_b[o][rk, cols], dctx[s][rq, cols]
-                prob = softmax(q, k, lengths[s][p])
-                dp = dot_nt(dc, v)
-                ds = (prob * (dp - jnp.sum(prob * dp, axis=-1, keepdims=True))).astype(BF16)
-                r_own[s][3][rq, cols] = (dot(ds, k) * SCALE).astype(BF16)
-                r_own[o][4][rk, cols] = (dot_tn(ds, q) * SCALE).astype(BF16)
-                r_own[o][5][rk, cols] = dot_tn(prob.astype(BF16), dc).astype(BF16)
-
-        loop(HEADS, body)
+                r_own[s][3][rq, c] = dq.astype(BF16)
+                r_own[o][4][rk, c] = dk.astype(BF16)
+                r_own[o][5][rk, c] = dv.astype(BF16)
+
+        loop(HEADS // HEAD_GROUP, body, 1)
         send_right(s, 3)
         send_right(o, 4)
         send_right(o, 5)
@@ -360,7 +400,7 @@
             v = dot(low[s][pl.ds(0, m), :], up_w[:, at(i, TILE)])
             half = 0.5 * (1.0 + lax.erf(v * (1.0 / math.sqrt(2.0))))
             r_own[s][0][pl.ds(0, m), c] = (v * half).astype(BF16)
-            slope[s][pl.ds(0, m), c] = (half + v * jnp.exp(-0.5 * v * v) * (1.0 / math.sqrt(2.0 * math.pi))).astype(BF16)
+            r_own[s][1][pl.ds(0, m), c] = (half + v * jnp.exp(-0.5 * v * v) * (1.0 / math.sqrt(2.0 * math.pi))).astype(BF16)
 
         loop(1024 // TILE, hidden)
 
@@ -379,7 +419,7 @@
         def body(i):
             c = pl.ds(pl.multiple_of(base + i * TILE, TILE), TILE)
             g = dot_nt(low[s][pl.ds(0, m), :], down_w[at(i, TILE), :])
-            r_own[s][1][pl.ds(0, m), c] = (g * slope[s][pl.ds(0, m), c].astype(F32)).astype(BF16)
+            r_own[s][1][pl.ds(0, m), c] = (g * r_own[s][1][pl.ds(0, m), c].astype(F32)).astype(BF16)
 
         loop(1024 // TILE, body)
 
@@ -413,13 +453,12 @@
 
     def step(name):
         if name == "i_qkv":
-            in_copies[0].wait()
+            wait(in_copies[0])
             project(x_t, m_t, weight("tk"), k_b[T])
             release("tk")
             project(x_t, m_t, weight("tv"), v_b[T])
             release("tv")
-            in_copies[1].wait()
-            spread(raw_i.at[0], x_i)
+            wait(in_copies[1])
             project(x_i, m_i, weight("iq"), q_b[I])
             release("iq")
         elif name == "i_attend":
@@ -431,8 +470,7 @@
             ffn(I, 0, weight("iu"), weight("id"))
             send_right(I, 0)
         elif name == "i_norm":
-            in_copies[3].wait()
-            spread(raw_i.at[1], u_i)
+            wait(in_copies[3])
             norm_two(I, u_i, u_i)
             gather_rows(u_i, res_i)
         elif name == "i_slope":
@@ -468,7 +506,7 @@
             if j == parts - 1:
                 send_right(T, 0)
         elif name == "t_norm":
-            in_copies[2].wait()
+            wait(in_copies[2])
             norm_two(T, u_t, res_t)
         elif name.startswith("t_slope"):
             j = int(name[-1])
@@ -558,18 +596,19 @@
     chunks = []
     for s, w in PRODUCED:
         for o in range(0, r_far[s][w].shape[1], CW):
-            chunks.append((s, w, o, "xy"[len(chunks) % 2], len([1 for c in chunks if c[0] == s])))
+            late = len(chunks) in LATE
+            chunks.append((s, w, o, "xy"[len(chunks) % 2], len([1 for c in chunks if c[0] == s]), late))
     n = len(chunks)
 
     def bufs(c):
         rows = pl.ds(0, d_of[chunks[c][0]] // (nz * ny * nx))
         return (
             g_b.at[c % G_RING, :, :, :, rows], r1_b.at[c % R_RING, :, :, rows], r2_b.at[c % R_RING, :, rows],
-            ru_b.at[c % Z_RING, :, rows], rd_b.at[c % Z_RING, :, rows],
+            ru_b.at[c % Z_RING, :, :, rows], rd_b.at[c % Z_RING, :, :, rows],
         )
 
     def compute(c):
-        s, w, o, way, _ = chunks[c]
+        s, w, o, way, _, _ = chunks[c]
         for copy, key in ((ex_left[s, LEFTS[w]], (0, s, LEFTS[w])), (ex_right[s, w], (1, s, w))):
             if key not in arrived:
                 arrived.add(key)
@@ -601,22 +640,34 @@
 
     def s2(c):
         g, _, r2 = bufs(c)[:3]
-        if chunks[c][3] == "x":
-            return remote(g.at[:, 1 - y, x], r2, st_s.at[1, c], st_r.at[1, c], nbr_y)
-        return remote(g.at[:, y, 1 - x], r2, st_s.at[1, c], st_r.at[1, c], nbr_x)
+        first, late = chunks[c][3] == "x", chunks[c][5]
+        far = (1 - y, x) if first else (y, 1 - x)
+        src, dst = (g.at[z, far[0], far[1]], r2.at[0]) if late else (g.at[:, far[0], far[1]], r2)
+        return remote(src, dst, st_s.at[1, c], st_r.at[1, c], nbr_y if first else nbr_x)
+
+    def blocks(c, t):
+        g, _, _, ru, rd = bufs(c)
+        if not chunks[c][5]:
+            return [(g.at[t, y, x], ru.at[t, 0], rd.at[t, 0])]
+        here = (lambda j: g.at[t, j, x]) if chunks[c][3] == "x" else (lambda j: g.at[t, y, j])
+        return [(here(j), ru.at[t, j], rd.at[t, j]) for j in range(2)]
+
+    def along(c, rest, buf):
+        g = bufs(c)[0]
+        if not chunks[c][5]:
+            return g.at[rest, y, x], buf.at[rest, 0]
+        return (g.at[rest, :, x] if chunks[c][3] == "x" else g.at[rest, y]), buf.at[rest]
 
     def up(c, k):
-        g, ru = bufs(c)[0], bufs(c)[3]
-        rest = pl.ds(k + 1, nz - 1 - k)
-        return remote(g.at[rest, y, x], ru.at[rest], st_s.at[2, c], st_r.at[2, c], dev(k + 1, y, x))
+        src, dst = along(c, pl.ds(k + 1, nz - 1 - k), bufs(c)[3])
+        return remote(src, dst, st_s.at[2, c], st_r.at[2, c], dev(k + 1, y, x))
 
     def down(c, k):
-        g, rd = bufs(c)[0], bufs(c)[4]
-        rest = pl.ds(0, k)
-        return remote(g.at[rest, y, x], rd.at[rest], st_s.at[3, c], st_r.at[3, c], dev(k - 1, y, x))
+        src, dst = along(c, pl.ds(0, k), bufs(c)[4])
+        return remote(src, dst, st_s.at[3, c], st_r.at[3, c], dev(k - 1, y, x))
 
     def swap(c):
-        s, w, o, _, k = chunks[c]
+        s, w, o, _, k, _ = chunks[c]
         out = w_out[s][w]
         half = out.shape[1] // 2
         return remote(
@@ -624,22 +675,7 @@
             st_s.at[4, c], st_r.at[4, c], partner,
         )
 
-    def stage2(c):
-        s1(c).wait_recv()
-        g, r1 = bufs(c)[:2]
-
-        def body(i):
-            for j in range(2):
-                add(g.at[i, j, x] if chunks[c][3] == "x" else g.at[i, y, j], r1.at[i, j])
-
-        loop(nz, body)
-        s2(c).start()
-
-    def stage3(c):
-        s2(c).wait_recv()
-        g, _, r2 = bufs(c)[:3]
-        loop(nz, lambda i: add(g.at[i, y, x], r2.at[i]))
-
+    def ends(c):
         @pl.when(z == 0)
         def _():
             up(c, 0).start()
@@ -648,69 +684,139 @@
         def _():
             down(c, nz - 1).start()
 
-    def hop(c, d):
+    def stage2(pair):
+        for c in pair:
+            s1(c).wait_recv()
+        for c in pair:
+            g, r1 = bufs(c)[:2]
+
+            def body(i):
+                for j in range(2):
+                    add(g.at[i, j, x] if chunks[c][3] == "x" else g.at[i, y, j], r1.at[i, j])
+
+            loop(nz, body)
+            if chunks[c][5]:
+                ends(c)
+            else:
+                s2(c).start()
+
+    def stage3(pair):
+        for c in pair:
+            s2(c).wait_recv()
+        for c in pair:
+            g, _, r2 = bufs(c)[:3]
+            loop(nz, lambda i: add(g.at[i, y, x], r2.at[i]))
+            ends(c)
+
+    def hop(pair, d):
+        for c in pair:
+
+            @pl.when(z == d)
+            def _(c=c):
+                up(c, d - 1).wait_recv()
+                for t in range(d + 1, nz):
+                    for here, below, _ in blocks(c, t):
+                        add(here, below)
+                up(c, d).start()
+
+            @pl.when(z == nz - 1 - d)
+            def _(c=c):
+                down(c, nz - d).wait_recv()
+                for t in range(0, nz - 1 - d):
+                    for here, _, above in blocks(c, t):
+                        add(here, above)
+                down(c, nz - 1 - d).start()
+
+    def last_hops(c, k):
+        if k == nz - 1:
+            up(c, k - 1).wait_recv()
+        if k == 0:
+            down(c, 1).wait_recv()
+
+    def z_total(c, k, j):
         g, _, _, ru, rd = bufs(c)
-
-        @pl.when(z == d)
-        def _():
-            up(c, d - 1).wait_recv()
-            for t in range(d + 1, nz):
-                add(g.at[t, y, x], ru.at[t])
-            up(c, d).start()
-
-        @pl.when(z == nz - 1 - d)
-        def _():
-            down(c, nz - d).wait_recv()
-            for t in range(0, nz - 1 - d):
-                add(g.at[t, y, x], rd.at[t])
-            down(c, nz - 1 - d).start()
-
-    def finish(c):
-        g, _, _, ru, rd = bufs(c)
-        s, w, o, _, idx = chunks[c]
-        out = w_out[s][w]
-        r, half = out.shape[0], out.shape[1] // 2
-        cols = pl.ds(pl.multiple_of(h * half + o, 128), CW)
-        for k in range(nz):
-
-            @pl.when(z == k)
-            def _(k=k):
-                if k == nz - 1:
-                    up(c, k - 1).wait_recv()
-                if k == 0:
-                    down(c, 1).wait_recv()
-                total = g[k, y, x].astype(F32)
-                if k > 0:
-                    total = total + ru[k].astype(F32)
-                if k < nz - 1:
-                    total = total + rd[k].astype(F32)
-                first, second = total[:r], total[r:]
-                out[:, cols] = jnp.where(h == 0, first, second)
-                f_b[s][idx] = jnp.where(h == 0, second, first)
-
-        swap(c).start()
-        s1(c).wait_send()
-        s2(c).wait_send()
-        for k in range(nz):
-
-            @pl.when(z == k)
-            def _(k=k):
-                if k < nz - 1:
-                    up(c, k).wait_send()
-                if k > 0:
-                    down(c, k).wait_send()
+        late, first = chunks[c][5], chunks[c][3] == "x"
+        lane = j if late else 0
+        row, col = (j, x) if late and first else (y, j) if late else (y, x)
+        total = g[k, row, col].astype(F32)
+        if k > 0:
+            total = total + ru[k, lane].astype(F32)
+        if k < nz - 1:
+            total = total + rd[k, lane].astype(F32)
+        return total
+
+    def fold(pair):
+        for c in pair:
+            far = 1 - y if chunks[c][3] == "x" else 1 - x
+            for k in range(nz):
+
+                @pl.when(z == k)
+                def _(c=c, k=k, far=far):
+                    last_hops(c, k)
+                    got = z_total(c, k, far).astype(BF16)
+                    g = bufs(c)[0]
+                    if chunks[c][3] == "x":
+                        g[k, far, x] = got
+                    else:
+                        g[k, y, far] = got
+
+            s2(c).start()
+
+    def finish(pair):
+        for c in pair:
+            s, w, o, way, idx, late = chunks[c]
+            out = w_out[s][w]
+            r, half = out.shape[0], out.shape[1] // 2
+            cols = pl.ds(pl.multiple_of(h * half + o, 128), CW)
+            if late:
+                s2(c).wait_recv()
+            for k in range(nz):
+
+                @pl.when(z == k)
+                def _(k=k):
+                    if not late:
+                        last_hops(c, k)
+                    total = z_total(c, k, y if way == "x" else x)
+                    if late:
+                        total = total + bufs(c)[2][0].astype(F32)
+                    first, second = total[:r], total[r:]
+                    out[:, cols] = jnp.where(h == 0, first, second)
+                    f_b[s][idx] = jnp.where(h == 0, second, first)
+
+            swap(c).start()
+            s1(c).wait_send()
+            s2(c).wait_send()
+            for k in range(nz):
+
+                @pl.when(z == k)
+                def _(k=k):
+                    if k < nz - 1:
+                        up(c, k).wait_send()
+                    if k > 0:
+                        down(c, k).wait_send()
 
     pairs = n // 2
-    small_from = 6
+    small_from = 9
+
+    def stage(p, lag):
+        pair = (2 * p, 2 * p + 1)
+        if lag == 0:
+            return stage2(pair)
+        if lag == nz:
+            return finish(pair)
+        for late in (True, False):
+            part = [c for c in pair if chunks[c][5] == late]
+            if late and lag == nz - 1:
+                fold(part)
+            elif not late and lag == 1:
+                stage3(part)
+            else:
+                hop(part, lag if late else lag - 1)
 
     def tick(t):
-        for lag, stage in (
-            (0, stage2), (1, stage3), *[(1 + d, functools.partial(hop, d=d)) for d in range(1, nz - 1)], (nz, finish)
-        ):
-            p = t - lag
-            if 0 <= p < pairs:
-                stage(2 * p)
-                stage(2 * p + 1)
+        for lag in range(nz, -1, -1):
+            if 0 <= t - lag < pairs:
+                stage(t - lag, lag)
         if small_from <= t < small_from + 5:
             small_step(t - small_from)
 
@@ -724,6 +830,15 @@
         copy.wait_send()
     for copy in small_copies:
         copy.wait_send()
+
+
+def hand_over(*refs):
+    n = len(refs) // 2
+    copies = [pltpu.make_async_copy(refs[i], refs[n + i], refs[-1].at[i]) for i in range(n)]
+    for c in copies:
+        c.start()
+    for c in copies:
+        c.wait()
 
 
 def layer(dims, lengths, states, upstream, weights, gains, shifts):
@@ -746,9 +861,9 @@
     act = lambda dt, width: [V((rows_of[s], width[s]), dt) for s in range(2)]
     scratch = [
         V((SLOTS, 1024, 1024), BF16),
-        V((mt, td), BF16), V((fixed, ti), BF16), V((2, pairs, regions, ti), BF16), V((mt, td), BF16), V((fixed, ti), BF16),
+        V((mt, td), BF16), V((fixed, ti), BF16),
         *act(BF16, (inner, inner)), *act(BF16, (inner, inner)), *act(BF16, (inner, inner)),
-        *act(F32, d_of), *act(F32, (128, 128)), *act(BF16, d_of), *act(BF16, (cols[0][1], cols[1][1])),
+        *act(F32, d_of), *act(F32, (128, 128)), *act(BF16, d_of),
         *act(F32, d_of), *act(BF16, (inner, inner)),
         *[V((4, 8, d), F32) for d in d_of],
         *[V((4, d, 512), BF16) for d in d_of],
@@ -757,11 +872,11 @@
         V((G_RING, nz, ny, nx, ti_blk, CW), BF16),
         V((R_RING, nz, 2, ti_blk, CW), BF16),
         V((R_RING, nz, ti_blk, CW), BF16),
-        V((Z_RING, nz, ti_blk, CW), BF16),
-        V((Z_RING, nz, ti_blk, CW), BF16),
+        V((Z_RING, nz, 2, ti_blk, CW), BF16),
+        V((Z_RING, nz, 2, ti_blk, CW), BF16),
         *[V((counts[s], d_of[s] // chips // 2, CW), F32) for s in range(2)],
         V((8, max(d_of)), F32), V((3, 8, max(d_of)), F32), V((2 + nz, 8, max(d_of)), F32),
-        DMA((4,)), DMA((SLOTS,)), DMA((20,)), DMA((20,)), DMA((5, n)), DMA((5, n)), DMA((2 + nz,)), DMA((2 + nz,)),
+        DMA((2 + 2 * pairs,)), DMA((SLOTS,)), DMA((20,)), DMA((20,)), DMA((5, n)), DMA((5, n)), DMA((2 + nz,)), DMA((2 + nz,)),
     ]
     hbm = pl.BlockSpec(memory_space=pl.ANY)
     vm = pl.BlockSpec(memory_space=pltpu.VMEM)
@@ -783,7 +898,15 @@
         ),
         name="co_layer",
     )(*lengths, xt, xi, ut, upstream[1], *weights[0], *weights[1], *gains, *shifts)
-    return got
+    n = len(got)
+    return pl.pallas_call(
+        hand_over,
+        out_shape=outs,
+        in_specs=[vm] * n,
+        out_specs=[hbm] * n,
+        scratch_shapes=[DMA((n,))],
+        name="hand_over",
+    )(*got)
 
 
 def matmul(row_values, weight):

time: 204 us -> 153 us (0.75)
  Pallas kernels: 186 us -> 152 us
  local copies, waits for them, and re-layouts: 16.5 us -> 0 us
    pallas_call x1, Pallas kernels: 186 us -> 148 us  [layer(): pl.pallas_call(functools.partial(layer_kernel, dims), out_shape=outs, in_...]
    unnamed x54 -> x0, local copies, waits for them, and re-layouts: 16.5 us -> none
    pallas_call x0 -> x1, Pallas kernels: none -> 3.88 us  [layer(): pl.pallas_call(hand_over, out_shape=outs, in_specs=[vm] * n, out_specs=[h...]
where the time goes in v2:
time: 153 us
  Pallas kernels  152 us (99%)
    pallas_call x1, Pallas kernels, layer(): pl.pallas_call(functools.partial(layer_kernel, dims), out_shape=outs, in_...  148 us
    pallas_call x1, Pallas kernels, layer(): pl.pallas_call(hand_over, out_shape=outs, in_specs=[vm] * n, out_specs=[h...  3.88 us

profile of v2, /device:TPU:0, one launch (start us, length us, event | category | flops | bytes accessed | tf_op | source)
XLA Modules:
  0.0 153.1 jit_solution(7229241940982706276)
XLA Ops:
  0.7 148.4 %co_layer.1 = (bf16[256,768]{1,0:T(8,128)(2,1)}, bf16[2,104,1024]{2,1,0:T(8,128)(2,1)}, bf16[256,768]{1,0:T(8,128)(2,1)}, bf16[2,104,1024]{2,1,0:T(8,128)(2,1)},...) custom-call(s32[4]{0:T(128)} %refs_0_.1, ...), custom_call_target="tpu_custom_call" | custom-call | tf_op jit(solution)/shard_map/co_layer/pallas_call | solution.py:890
  149.1 3.9 %hand_over.1 = (bf16[256,768]{1,0:T(8,128)(2,1)}, bf16[2,104,1024]{2,1,0:T(8,128)(2,1)}, bf16[256,768]{1,0:T(8,128)(2,1)}, bf16[2,104,1024]{2,1,0:T(8,128)(2,1)}...) custom-call(bf16[256,768]{1,0:T(8,128)(2,1)} %get-tuple-element.60.r, ...), custom_call_target="tpu_custom_call" | custom-call | tf_op jit(solution)/shard_map/hand_over/pallas_call | solution.py:902

commit v3 on v2

--- a/solution.py
+++ b/solution.py
@@ -25,14 +25,21 @@
 UNROLL = 2
 HEAD_GROUP = 2
 G_RING, R_RING, Z_RING = 12, 12, 12
-LATE = (1, 2, 5, 6, 8, 11, 13, 14, 16, 17, 19, 20, 23, 24, 25, 26, 28, 29)
-PRODUCED = ((1, 0), (1, 1), (1, 2), (0, 0), (0, 1), (0, 2), (1, 3), (0, 4), (0, 5), (0, 3), (1, 4), (1, 5))
+LATE = (0, 3, 6, 9, 10, 13, 15, 16, 19, 20, 23, 24, 25, 26, 29)
+PRODUCED = ((1, 0), (1, 1), (1, 2), (0, 0), (0, 1), (0, 2), (1, 3), (0, 4), (0, 5), (1, 4), (1, 5), (0, 3))
+SMALL_FROM = 5
+STEPS = (
+    "i_qkv", "i_attend", "i_out", "i_ffn", "i_norm", "i_slope", "i_branch", "i_context", "t_q", "t_kv", "t_attend",
+    "t_out", "t_ffn0", "t_ffn1", "t_ffn2", "t_norm", "t_slope0", "t_slope1", "t_slope2", "t_branch", "i_back",
+    "t_context", "t_back", "i_final", "t_final",
+)
 SEQUENCE = (
-    "i_qkv", "i_attend", "i_out", "i_ffn", "i_norm", "A0", "i_slope", "i_branch", "i_context", "A1", "t_q", "t_kv",
-    "t_attend", "T0", "A2", "t_out", "t_ffn0", "t_ffn1", "T1", "t_ffn2", "t_norm", "A3", "T2", "t_slope0", "A4", "T3",
-    "A5", "t_slope1", "t_slope2", "T4", "A6", "t_branch", "T5", "A7", "T6", "A8", "i_back", "T7", "A9", "t_context",
-    "T8", "A10", "t_back", "T9", "i_final", "A11", "t_final", "T10", "A12", "T11", "A13", "T12", "A14", "T13", "T14",
-    "A15", "T15", "T16", "T17", "T18", "T19",
+    -1, -1, -1, -1, -1, 0, -1, -1, 1, -1, 2, -1, -1, -1, -1, 100, -1, -1, 200, 300, -1, 101, -1, 3, 201, 4, -1, -1,
+    102, 301, -1, 400, 202, 103, 5, 302, 500, 203, 104, 6, 401, -1, 600, 303, 204, 7, 402, 501, -1, 601, 403, 304,
+    502, 700, 8, -1, 503, 602, 404, 800, 701, 9, 900, 603, 504, 10, 702, 801, 703, 901, 604, 11, 802, 1000, -1, 803,
+    1100, -1, 902, 704, 12, 804, 1001, -1, 1101, 1200, 903, 13, 1002, 904, 1300, 1003, 14, 1102, 1004, 1201, 1400, 15,
+    1103, 1301, 1202, 1500, 1401, 1302, 1203, 1600, 1501, 1402, 1601, 1303, 1502, 1602, 1104, 1403, 1503, 1204, 1603,
+    1304, 1404, 1504, 1604,
 )
 
 
@@ -91,7 +98,7 @@
     g_b, r1_b, r2_b, ru_b, rd_b = take(5)
     f_b = take(2)
     small, sv, sr = take(3)
-    in_sem, w_sem, ex_s, ex_r, st_s, st_r, sm_s, sm_r = take(8)
+    in_sem, w_sem, ex_s, ex_r, st_s, st_r, sw_s, sw_r, sm_s, sm_r = take(10)
     assert not refs
     u_t, u_i = dctx[0].at[:, pl.ds(0, x_t.shape[1])], dctx[1]
 
@@ -544,12 +551,17 @@
             back_add(T, r_own[T][3], all_cols, weight("tq"))
             release("tq")
             final(T, sg_t)
-        elif name[0] == "A":
-            for c in (2 * int(name[1:]), 2 * int(name[1:]) + 1):
+
+    def token(k):
+        if k < 100:
+            for c in (2 * k, 2 * k + 1):
                 compute(c)
                 s1(c).start()
-        else:
-            tick(int(name[1:]))
+            return
+        p, lag = k // 100 - 1, k % 100
+        stage(p, lag)
+        if lag == nz and SMALL_FROM <= p < SMALL_FROM + 5:
+            small_step(p - SMALL_FROM)
 
     small_copies = []
 
@@ -635,15 +647,15 @@
     def s1(c):
         g, r1 = bufs(c)[:2]
         if chunks[c][3] == "x":
-            return remote(g.at[:, :, 1 - x], r1, st_s.at[0, c], st_r.at[0, c], nbr_x)
-        return remote(g.at[:, 1 - y], r1, st_s.at[0, c], st_r.at[0, c], nbr_y)
+            return remote(g.at[:, :, 1 - x], r1, st_s.at[0, c % G_RING], st_r.at[0, c % G_RING], nbr_x)
+        return remote(g.at[:, 1 - y], r1, st_s.at[0, c % G_RING], st_r.at[0, c % G_RING], nbr_y)
 
     def s2(c):
         g, _, r2 = bufs(c)[:3]
         first, late = chunks[c][3] == "x", chunks[c][5]
         far = (1 - y, x) if first else (y, 1 - x)
         src, dst = (g.at[z, far[0], far[1]], r2.at[0]) if late else (g.at[:, far[0], far[1]], r2)
-        return remote(src, dst, st_s.at[1, c], st_r.at[1, c], nbr_y if first else nbr_x)
+        return remote(src, dst, st_s.at[1, c % G_RING], st_r.at[1, c % G_RING], nbr_y if first else nbr_x)
 
     def blocks(c, t):
         g, _, _, ru, rd = bufs(c)
@@ -660,11 +672,11 @@
 
     def up(c, k):
         src, dst = along(c, pl.ds(k + 1, nz - 1 - k), bufs(c)[3])
-        return remote(src, dst, st_s.at[2, c], st_r.at[2, c], dev(k + 1, y, x))
+        return remote(src, dst, st_s.at[2, c % G_RING], st_r.at[2, c % G_RING], dev(k + 1, y, x))
 
     def down(c, k):
         src, dst = along(c, pl.ds(0, k), bufs(c)[4])
-        return remote(src, dst, st_s.at[3, c], st_r.at[3, c], dev(k - 1, y, x))
+        return remote(src, dst, st_s.at[3, c % G_RING], st_r.at[3, c % G_RING], dev(k - 1, y, x))
 
     def swap(c):
         s, w, o, _, k, _ = chunks[c]
@@ -672,7 +684,7 @@
         half = out.shape[1] // 2
         return remote(
             f_b[s].at[k], out.at[:, pl.ds(pl.multiple_of(h * half + o, 128), CW)],
-            st_s.at[4, c], st_r.at[4, c], partner,
+            sw_s.at[c], sw_r.at[c], partner,
         )
 
     def ends(c):
@@ -795,8 +807,6 @@
                     if k > 0:
                         down(c, k).wait_send()
 
-    pairs = n // 2
-    small_from = 9
 
     def stage(p, lag):
         pair = (2 * p, 2 * p + 1)
@@ -813,15 +823,12 @@
             else:
                 hop(part, lag if late else lag - 1)
 
-    def tick(t):
-        for lag in range(nz, -1, -1):
-            if 0 <= t - lag < pairs:
-                stage(t - lag, lag)
-        if small_from <= t < small_from + 5:
-            small_step(t - small_from)
-
-    for name in SEQUENCE:
-        step(name)
+    names = iter(STEPS)
+    for k in SEQUENCE:
+        if k < 0:
+            step(next(names))
+        else:
+            token(k)
 
     for c in range(n):
         swap(c).wait_recv()
@@ -876,7 +883,7 @@
         V((Z_RING, nz, 2, ti_blk, CW), BF16),
         *[V((counts[s], d_of[s] // chips // 2, CW), F32) for s in range(2)],
         V((8, max(d_of)), F32), V((3, 8, max(d_of)), F32), V((2 + nz, 8, max(d_of)), F32),
-        DMA((2 + 2 * pairs,)), DMA((SLOTS,)), DMA((20,)), DMA((20,)), DMA((5, n)), DMA((5, n)), DMA((2 + nz,)), DMA((2 + nz,)),
+        DMA((2 + 2 * pairs,)), DMA((SLOTS,)), DMA((20,)), DMA((20,)), DMA((4, G_RING)), DMA((4, G_RING)), DMA((n,)), DMA((n,)), DMA((2 + nz,)), DMA((2 + nz,)),
     ]
     hbm = pl.BlockSpec(memory_space=pl.ANY)
     vm = pl.BlockSpec(memory_space=pltpu.VMEM)

time: 153 us -> 149 us (0.974)
  Pallas kernels: 152 us -> 148 us
    pallas_call x1, Pallas kernels: 148 us -> 144 us  [layer(): pl.pallas_call(functools.partial(layer_kernel, dims), out_shape=outs, in_...]
where the time goes in v3:
time: 149 us
  Pallas kernels  148 us (99%)
    pallas_call x1, Pallas kernels, layer(): pl.pallas_call(functools.partial(layer_kernel, dims), out_shape=outs, in_...  144 us
    pallas_call x1, Pallas kernels, layer(): pl.pallas_call(hand_over, out_shape=outs, in_specs=[vm] * n, out_specs=[h...  3.88 us

profile of v3, /device:TPU:0, one launch (start us, length us, event | category | flops | bytes accessed | tf_op | source)
XLA Modules:
  0.0 148.8 jit_solution(8451558408969930033)
XLA Ops:
  0.7 144.1 %co_layer.1 = (bf16[256,768]{1,0:T(8,128)(2,1)}, bf16[2,104,1024]{2,1,0:T(8,128)(2,1)}, bf16[256,768]{1,0:T(8,128)(2,1)}, bf16[2,104,1024]{2,1,0:T(8,128)(2,1)},...) custom-call(s32[4]{0:T(128)} %refs_0_.1, ...), custom_call_target="tpu_custom_call" | custom-call | tf_op jit(solution)/shard_map/co_layer/pallas_call | solution.py:897
  144.7 3.9 %hand_over.1 = (bf16[256,768]{1,0:T(8,128)(2,1)}, bf16[2,104,1024]{2,1,0:T(8,128)(2,1)}, bf16[256,768]{1,0:T(8,128)(2,1)}, bf16[2,104,1024]{2,1,0:T(8,128)(2,1)}...) custom-call(bf16[256,768]{1,0:T(8,128)(2,1)} %get-tuple-element.60.r, ...), custom_call_target="tpu_custom_call" | custom-call | tf_op jit(solution)/shard_map/hand_over/pallas_call | solution.py:909

commit v4 on v3

--- a/solution.py
+++ b/solution.py
@@ -25,8 +25,8 @@
 UNROLL = 2
 HEAD_GROUP = 2
 G_RING, R_RING, Z_RING = 12, 12, 12
-LATE = (0, 3, 6, 9, 10, 13, 15, 16, 19, 20, 23, 24, 25, 26, 29)
-PRODUCED = ((1, 0), (1, 1), (1, 2), (0, 0), (0, 1), (0, 2), (1, 3), (0, 4), (0, 5), (1, 4), (1, 5), (0, 3))
+LATE = (0, 6, 9, 10, 13, 15, 16, 19, 20, 22, 23, 24, 25, 26, 27)
+PRODUCED = ((1, 0), (1, 1), (1, 2), (0, 0), (0, 1), (0, 2), (1, 3), (0, 4), (0, 5), (0, 3), (1, 4), (1, 5))
 SMALL_FROM = 5
 STEPS = (
     "i_qkv", "i_attend", "i_out", "i_ffn", "i_norm", "i_slope", "i_branch", "i_context", "t_q", "t_kv", "t_attend",
@@ -34,12 +34,12 @@
     "t_context", "t_back", "i_final", "t_final",
 )
 SEQUENCE = (
-    -1, -1, -1, -1, -1, 0, -1, -1, 1, -1, 2, -1, -1, -1, -1, 100, -1, -1, 200, 300, -1, 101, -1, 3, 201, 4, -1, -1,
-    102, 301, -1, 400, 202, 103, 5, 302, 500, 203, 104, 6, 401, -1, 600, 303, 204, 7, 402, 501, -1, 601, 403, 304,
-    502, 700, 8, -1, 503, 602, 404, 800, 701, 9, 900, 603, 504, 10, 702, 801, 703, 901, 604, 11, 802, 1000, -1, 803,
-    1100, -1, 902, 704, 12, 804, 1001, -1, 1101, 1200, 903, 13, 1002, 904, 1300, 1003, 14, 1102, 1004, 1201, 1400, 15,
-    1103, 1301, 1202, 1500, 1401, 1302, 1203, 1600, 1501, 1402, 1601, 1303, 1502, 1602, 1104, 1403, 1503, 1204, 1603,
-    1304, 1404, 1504, 1604,
+    -1, -1, -1, -1, -1, 0, -1, 1, -1, -1, -1, -1, 2, -1, -1, 100, 200, -1, -1, 300, -1, 101, -1, 3, 201, -1, 102, 4,
+    -1, 301, -1, 103, 400, 202, 5, -1, 302, 203, 104, 500, 401, 6, 204, 600, 7, 402, 501, 303, -1, 403, 700, 304, 502,
+    601, 8, -1, 701, 800, 404, 503, 9, 602, 504, 900, 801, 603, 702, 10, 901, 802, 1000, 703, 604, 11, 803, 902, 704,
+    12, 1100, 1001, -1, 903, 1002, 804, 1200, 13, 1101, 1003, 904, 14, 1201, 1300, 1004, 15, 1102, 1301, 1400, 1202,
+    1500, -1, 1103, 1600, 1401, 1501, 1203, 1302, 1601, 1303, 1104, 1402, 1204, 1502, 1403, 1304, 1602, 1404, -1,
+    1503, 1603, 1504, 1604,
 )
 
 

time: 149 us -> 148 us (level)
  no operation moved by 1% of the time
where the time goes in v4:
time: 148 us
  Pallas kernels  147 us (99%)
    pallas_call x1, Pallas kernels, layer(): pl.pallas_call(functools.partial(layer_kernel, dims), out_shape=outs, in_...  143 us
    pallas_call x1, Pallas kernels, layer(): pl.pallas_call(hand_over, out_shape=outs, in_specs=[vm] * n, out_specs=[h...  3.88 us

profile of v4, /device:TPU:0, one launch (start us, length us, event | category | flops | bytes accessed | tf_op | source)
XLA Modules:
  0.0 147.8 jit_solution(4259324422288296377)
XLA Ops:
  0.7 143.1 %co_layer.1 = (bf16[256,768]{1,0:T(8,128)(2,1)}, bf16[2,104,1024]{2,1,0:T(8,128)(2,1)}, bf16[256,768]{1,0:T(8,128)(2,1)}, bf16[2,104,1024]{2,1,0:T(8,128)(2,1)},...) custom-call(s32[4]{0:T(128)} %refs_0_.1, ...), custom_call_target="tpu_custom_call" | custom-call | tf_op jit(solution)/shard_map/co_layer/pallas_call | solution.py:897
  143.8 3.9 %hand_over.1 = (bf16[256,768]{1,0:T(8,128)(2,1)}, bf16[2,104,1024]{2,1,0:T(8,128)(2,1)}, bf16[256,768]{1,0:T(8,128)(2,1)}, bf16[2,104,1024]{2,1,0:T(8,128)(2,1)}...) custom-call(bf16[256,768]{1,0:T(8,128)(2,1)} %get-tuple-element.60.r, ...), custom_call_target="tpu_custom_call" | custom-call | tf_op jit(solution)/shard_map/hand_over/pallas_call | solution.py:909
